TPU v7x, 768 devices: a whole 4x8x12 slice. The times are simulated.
768 devices in a mesh: row: 64 (over x, y, core), col: 12 (over z).
Axes of the slice: x: 4, y: 8, z: 12, core: 2. Of those that a mesh axis runs over, the one named last changes fastest.
Arguments:
- points: bfloat16 [786432, 256], P(('row', 'col'))
- centres: bfloat16 [2048, 256], replicated, may hold values from -1.5 to 1.5
- picks: int32 [2, 1024], replicated, may hold values from 0 to 786431, as said below
- assign_pts: int32 [786432], P(('row', 'col')), may hold values from 0 to 4095
- cand_assign: int32 [4096, 1], replicated, may hold values from 0 to 1023
Outputs:
- relative_cost: float32 [786432], P(('row', 'col'))
- new_centres: float32 [1024, 256], P('row')
Inputs may be any that keep to these rules, and one draw needn't show every extreme that they name: Each row of picks holds 1024 distinct point indices; in each row the points of one device, the block of 1024 consecutive indices, appear at most 3 times, and some device appears exactly 3 times.
All inputs are finite; a program needn't handle non-finite values.
Results may differ from a plain program's by a relative error of at most 0.0005.
Values may be sent and summed in bfloat16 or wider, within the bound.
A program may use at most 32 MiB of HBM per device.

v0:
```python
import jax
import jax.numpy as jnp
from jax import lax
from jax.sharding import PartitionSpec as P

K_FINAL = 1024


def squared_norms(matrix):
    return jnp.einsum("nd,nd->n", matrix, matrix, preferred_element_type=jnp.float32)


def nearest_distance(points, point_norms, cand_table, keep_mask):
    total_rows = cand_table.shape[0]
    block_rows = min(512, total_rows)
    blocks = cand_table.reshape(-1, block_rows, cand_table.shape[1])
    keep_blocks = keep_mask.reshape(-1, block_rows)

    def visit_block(carried, inputs):
        block_table, block_keep = inputs
        products = lax.dot_general(
            points, block_table, (((1,), (1,)), ((), ())), preferred_element_type=jnp.float32
        )
        distance = point_norms[:, None] + squared_norms(block_table)[None, :] - 2.0 * products
        distance = jnp.where(block_keep[None, :], distance, jnp.inf)
        return (jnp.minimum(carried, jnp.min(distance, axis=1)), None)

    start_value = jnp.full((points.shape[0],), jnp.inf, jnp.float32)
    result, unused = lax.scan(visit_block, start_value, (blocks, keep_blocks))
    return result


def shards(points, centres, picks, assign_pts, cand_assign):
    point_count = points.shape[0]
    feature_count = points.shape[1]
    device_count = lax.axis_size("row") * lax.axis_size("col")
    device_index = lax.axis_index("row") * lax.axis_size("col") + lax.axis_index("col")
    round_count, sample_count = picks.shape
    first_count = centres.shape[0]
    cand_count = first_count + round_count * sample_count
    local_index = picks - device_index * point_count
    owned = (local_index >= 0) & (local_index < point_count)
    clipped = jnp.clip(local_index, 0, point_count - 1)
    tally = jax.ops.segment_sum(
        jnp.ones((point_count,), jnp.float32), assign_pts, num_segments=cand_count
    )
    point_norms = squared_norms(points)
    picked = jnp.where(
        owned[:, :, None], points[clipped].astype(jnp.float32), jnp.zeros((), jnp.float32)
    )
    summed = lax.psum(picked.reshape(-1, feature_count), ("row", "col"))
    cand_table = jnp.concatenate([centres, summed.astype(jnp.bfloat16)], axis=0)
    slot_ids = jnp.arange(cand_count, dtype=jnp.int32)
    keep_mask = slot_ids >= 0
    nearest = nearest_distance(points, point_norms, cand_table, keep_mask)
    best = jnp.maximum(nearest, 0.0)
    total_cost, counts = lax.psum((jnp.sum(best), tally), ("row", "col"))
    relative_cost = best * (point_count * device_count) / total_cost
    safe_ids = jnp.clip(slot_ids, 0, cand_count - 1)
    weights = jnp.where(keep_mask, 1.0 + counts[safe_ids], 0.0)
    owners = cand_assign[:, 0][safe_ids]
    block_final = K_FINAL // lax.axis_size("row")
    targets = lax.axis_index("row") * block_final + jnp.arange(block_final, dtype=jnp.int32)
    member = jnp.where(owners[None, :] == targets[:, None], weights[None, :], 0.0)
    numerator = jnp.dot(member, cand_table.astype(jnp.float32), precision=lax.Precision.HIGHEST)
    denominator = jnp.sum(member, axis=1)
    new_centres = numerator / denominator[:, None]
    return (relative_cost, new_centres)


def solution(mesh):
    placed = (P(("row", "col"), None), P(), P(), P(("row", "col")), P())
    return jax.shard_map(
        shards,
        mesh=mesh,
        in_specs=placed,
        out_specs=(P(("row", "col")), P("row", None)),
        check_vma=False,
    )
```

profile of v0, /device:TPU:1, one launch (start us, length us, event | category | flops | bytes accessed | tf_op | source)
XLA Modules:
  0.0 315.4 jit_solution(14783939888377154478)
XLA Ops:
  0.6 0.0 copy-start
  0.7 0.7 fusion.12
  1.4 7.8 %gather_fusion = bf16[2048,256]{1,0:T(8,128)(2,1)S(1)} fusion(bf16[1024,256]{1,0:T(8,128)(2,1)} %param.7, s32[2048]{0:T(1024)S(1)} %bitcast_clamp_fusion), kind=kCustom, calls=%fused_computation | custom fusion | bytes 2105344 | tf_op jit(solution)/shard_map/gather | solution.py:49
  9.2 0.3 convert_select_fusion
  9.6 134.8 %all-reduce.2 = bf16[2048,256]{1,0:T(8,128)(2,1)} all-reduce(f32[2048,256]{1,0:T(8,128)S(1)} %convert_select_fusion), channel_id=1, replica_groups=mesh['row'=64,'col'=12] {'row','col'}, use_global_device_ids=true, to_apply=%region_0.1 | all-reduce | flops 524288 | bytes 3145728 | tf_op jit(solution)/shard_map/psum | solution.py:51
  144.3 1.7 pad_maximum_fusion
  146.1 0.2 fusion.5
  146.3 5.5 %while.12 = (s32[]{:T(128)}, f32[1024]{0:T(1024)S(1)}, f32[1024]{0:T(1024)S(1)}, bf16[8,512,256]{2,1,0:T(8,128)(2,1)S(1)}, bf16[1024,256]{1,0:T(8,128)(2,1)S(1)}, /*index=5*/s32[]{:T(128)}, s32[]{:T(128)}) while((s32[]{:T(128)}, f32[1024]{0:T(1024)S(1)}, f32[1024]{0:T(1024)S(1)}, bf16[8,512,256]{2,1,0:T(8,128)(2,1)S(1)}, ...), condition=%wide.region_3.4_spmd.clone, body=%wide.region_1.3_spmd.clone.sunk | while | flops 270926336 | bytes 1073247 | solution.py:29
  146.3 0.2 fusion.23
  146.5 0.5 fusion.24
  147.0 0.2 fusion.23
  147.1 0.5 fusion.24
  147.7 0.2 fusion.23
  147.8 0.5 fusion.24
  148.4 0.2 fusion.23
  148.5 0.5 fusion.24
  149.0 0.2 fusion.23
  149.2 0.5 fusion.24
  149.7 0.2 fusion.23
  149.9 0.5 fusion.24
  150.4 0.2 fusion.23
  150.6 0.5 fusion.24
  151.1 0.2 fusion.23
  151.2 0.5 fusion.24
  151.8 0.6 maximum_reduce_fusion
  152.4 6.1 %scatter_custom_fusion = f32[4096]{0:T(1024)S(1)} fusion(s32[1024]{0:T(1024)} %param.10, f32[1024]{0:T(1024)S(1)} %broadcast.73, f32[]{:T(128)} %constant.30.clone.1), kind=kCustom, calls=%fused_computation.31 | custom fusion | flops 1024 | bytes 16896 | tf_op jit(solution)/shard_map/scatter-add | solution.py:44
  158.4 107.7 %all-reduce = (f32[]{:T(128)}, f32[4096]{0:T(1024)S(1)}) all-reduce(f32[]{:T(128)} %maximum_reduce_fusion, f32[4096]{0:T(1024)S(1)} %scatter_custom_fusion), channel_id=1, replica_groups=mesh['row'=64,'col'=12] {'row','col'}, use_global_device_ids=true, to_apply=%region_5.6 | all-reduce | flops 4097 | bytes 32776 | tf_op jit(solution)/shard_map/psum | solution.py:57
  266.2 23.0 %gather_fusion.2 = f32[4096]{0:T(1024)S(1)} fusion(f32[4096]{0:T(1024)S(1)} %get-tuple-element.79, s32[4096]{0:T(1024)S(1)} %broadcast_clamp_fusion), kind=kCustom, calls=%fused_computation.2 | custom fusion | bytes 49152 | tf_op jit(solution)/shard_map/gather | solution.py:60
  289.3 23.0 %gather_fusion.1 = s32[4096]{0:T(1024)S(1)} fusion(s32[4096]{0:T(1024)S(1)} %bitcast.24, s32[4096]{0:T(1024)S(1)} %broadcast_clamp_fusion), kind=kCustom, calls=%fused_computation.1 | custom fusion | bytes 49152 | tf_op jit(solution)/shard_map/gather | solution.py:61
  312.3 0.2 select_reduce_fusion
  312.6 1.6 convolution_divide_fusion
  314.2 1.3 multiply_divide_fusion
  (26 shorter events, 0.1 us)
Async XLA Ops:
  0.6 288.6 %copy-start = (s32[4096,1]{0,1:T(1,128)S(1)}, s32[4096,1]{0,1:T(1,128)}, u32[]{:S(2)}) copy-start(s32[4096,1]{0,1:T(1,128)} %param.11) | copy-start | bytes 49156
  1.4 7.8 %copy-start.4 = (s32[2,1024]{1,0:T(2,128)S(1)}, s32[2,1024]{1,0:T(2,128)}, u32[]{:S(2)}) copy-start(s32[2,1024]{1,0:T(2,128)} %param.9) | copy-start | bytes 24580
  144.3 1.8 copy-start.1
  289.3 23.3 %copy-start.2 = (bf16[2048,256]{1,0:T(8,128)(2,1)S(1)}, bf16[2048,256]{1,0:T(8,128)(2,1)}, u32[]{:S(2)}) copy-start(bf16[2048,256]{1,0:T(8,128)(2,1)} %all-reduce.2) | copy-start | bytes 3145732
  289.3 23.3 %copy-start.3 = (bf16[2048,256]{1,0:T(8,128)(2,1)S(1)}, bf16[2048,256]{1,0:T(8,128)(2,1)}, u32[]{:S(2)}) copy-start(bf16[2048,256]{1,0:T(8,128)(2,1)} %param.8) | copy-start | bytes 3145732
where the time goes:
time: 316 us; the launch traced here: 315 us
  blocking collectives  242 us (77%)
  local copies, waits for them, and re-layouts  53.9 us (17%)
  other arithmetic  12.5 us (4%)
  matrix products  5.48 us (2%)
    psum x1, blocking collectives, shards(): summed = lax.psum(picked.reshape(-1, feature_count), ('row', 'col'))  135 us
    psum x1, blocking collectives, shards(): total_cost, counts = lax.psum((jnp.sum(best), tally), ('row', 'col'))  108 us
    gather x1, local copies, waits for them, and re-layouts, shards(): weights = jnp.where(keep_mask, 1.0 + counts[safe_ids], 0.0)  23 us
    gather x1, local copies, waits for them, and re-layouts, shards(): owners = cand_assign[:, 0][safe_ids]  23 us
    gather x1, local copies, waits for them, and re-layouts, shards(): points[clipped].astype(jnp.float32)  7.75 us

commit v1 on v0

v1 whole, which is shorter than its diff:
```python
import functools
import jax
import jax.numpy as jnp
from jax import lax
from jax.experimental import pallas as pl
from jax.experimental.pallas import tpu as pltpu
from jax.sharding import PartitionSpec as P

K_FINAL = 1024
CORES = 2
CAP = 3
D = 256
F32, BF16, I32 = jnp.float32, jnp.bfloat16, jnp.int32
MESH = pl.DeviceIdType.MESH
BIG = 3.0e38
FAR = 1 << 20


def split3(value):
    high = value.astype(BF16)
    rest = value - high.astype(F32)
    middle = rest.astype(BF16)
    low = (rest - middle.astype(F32)).astype(BF16)
    return high, middle, low


def contract_last(left, right):
    return lax.dot_general(left, right, (((1,), (1,)), ((), ())), preferred_element_type=F32)


def near_first(size):
    return sorted(range(1, size), key=lambda step: (min(step, size - step), step))


def kernel(nx, ny, nz, npts,
           picks_ref, owner_ref, assign_ref, points_hbm, centres_hbm,
           cost_ref, final_ref,
           pts, pts2, cen, picked, zbuf, big, nearest, meta,
           hist, hist_x, hist_z, hist_y, counts,
           tot_x, tot_y, tot_z, local_sem,
           zs, zr, ys, yr, xs, xr, cs, cr,
           hxs, hxr, hzs, hzr, hys, hyr, has, har,
           txs, txr, tys, tyr, tzs, tzr):
    row = lax.axis_index("row")
    z = lax.axis_index("col")
    core = lax.rem(row, CORES)
    y = lax.rem(row // CORES, ny)
    x = row // (CORES * ny)
    me = row * nz + z
    slots = 2 * CAP
    rows = nz * slots
    blk = big.shape[3]
    nxc = nx * CORES

    def peer(ox=0, oy=0, oc=0, oz=0):
        px = lax.rem(x + ox, nx)
        py = lax.rem(y + oy, ny)
        pc = lax.rem(core + oc, CORES)
        return ((px * ny + py) * CORES + pc, lax.rem(z + oz, nz))

    def send(src, dst, ssem, rsem, device):
        copy = pltpu.make_async_remote_copy(
            src_ref=src, dst_ref=dst, send_sem=ssem, recv_sem=rsem,
            device_id=device, device_id_type=MESH)
        copy.start()
        return copy

    load_points = pltpu.make_async_copy(points_hbm, pts, local_sem.at[0])
    load_centres = pltpu.make_async_copy(centres_hbm, cen, local_sem.at[1])
    load_points.start()
    load_centres.start()

    xc_steps = [(ox, oc) for ox in range(nx) for oc in range(CORES) if ox or oc]
    barrier = pltpu.get_barrier_semaphore()
    peers = [peer(oz=o) for o in range(1, nz)] + [peer(oy=o) for o in range(1, ny)]
    peers += [peer(ox=ox, oc=oc) for ox, oc in xc_steps]
    for other in peers:
        pl.semaphore_signal(barrier, inc=1, device_id=other, device_id_type=MESH)

    for r in range(2):
        for b in range(8):
            picked[r * 8 + b:r * 8 + b + 1, :] = picks_ref[r:r + 1, b * 128:(b + 1) * 128]
    sub = lax.broadcasted_iota(I32, (8, 128), 0)
    lane = lax.broadcasted_iota(I32, (8, 128), 1)
    local_ids, codes = [], []
    for r in range(2):
        p = picked[r * 8:(r + 1) * 8, :]
        local = p - me * 1024
        own = (local >= 0) & (local < 1024)
        local = jnp.where(own, local, FAR)
        ids = r * 1024 + sub * 128 + lane
        code = ids * 1024 + owner_ref[16 + r * 8:24 + r * 8, :] + 1
        for s in range(CAP):
            first = jnp.min(jnp.min(local, axis=1, keepdims=True), axis=0, keepdims=True)
            hit = (local == first) & (local < FAR)
            coded = jnp.where(hit, code, 0)
            codes.append(jnp.max(jnp.max(coded, axis=1, keepdims=True), axis=0, keepdims=True))
            local_ids.append(first)
            local = jnp.where(local == first, FAR, local)
    slot_row = lax.broadcasted_iota(I32, (8, 1024), 0)
    point_lane = lax.broadcasted_iota(I32, (8, 1024), 1)
    want = jnp.full((8, 1024), FAR, I32)
    for s in range(slots):
        want = jnp.where(slot_row == s, local_ids[s], want)
    choose = jnp.where(want == point_lane, 1.0, 0.0)
    choose16 = jnp.concatenate([choose, jnp.zeros((8, 1024), F32)], axis=0).astype(BF16)
    lane1 = lax.broadcasted_iota(I32, (1, 128), 1)
    lane_dev = (lane1 * 43691) >> 18
    lane_slot = lane1 - lane_dev * slots
    code_row = jnp.zeros((1, 128), I32)
    for s in range(slots):
        code_row = jnp.where(lane_slot == s, codes[s], code_row)
    digit_a = (code_row & 255).astype(F32)
    digit_b = ((code_row >> 8) & 255).astype(F32)
    digit_c = (code_row >> 16).astype(F32)
    load_points.wait()
    load_centres.wait()
    mine = jnp.dot(choose16, pts[...], preferred_element_type=F32)[:8, :]
    slot_col = lax.broadcasted_iota(I32, (8, D), 0)
    filled = jnp.zeros((8, D), I32)
    for s in range(slots):
        filled = jnp.where(slot_col == s, jnp.broadcast_to(local_ids[s], (8, D)), filled)
    spare = jnp.broadcast_to(cen[0:16, :].astype(F32)[0:1, :], (8, D))
    mine = jnp.where(filled >= FAR, spare, mine)
    row_six = jnp.concatenate([digit_a, digit_b], axis=1)
    row_seven = jnp.concatenate([digit_c, digit_c], axis=1)
    mine = jnp.where(slot_col == slots, jnp.broadcast_to(row_six, (8, D)), mine)
    mine = jnp.where(slot_col == slots + 1, jnp.broadcast_to(row_seven, (8, D)), mine)
    zbuf[z] = mine.astype(BF16)

    pl.semaphore_wait(barrier, len(peers))

    sent = []
    zcopies = {}
    for o in near_first(nz)[::-1]:
        copy = send(zbuf.at[z], zbuf.at[z], zs.at[o], zr.at[o], peer(oz=o))
        sent.append(copy)

    acc = jnp.zeros((32, 128), F32)
    hi_iota = lax.broadcasted_iota(I32, (32, 128), 0)
    lo_iota = lax.broadcasted_iota(I32, (128, 128), 0)
    for b in range(8):
        a = assign_ref[b:b + 1, :]
        left = jnp.where(hi_iota == (a >> 7), 1.0, 0.0).astype(BF16)
        right = jnp.where(lo_iota == (a & 127), 1.0, 0.0).astype(BF16)
        acc = acc + contract_last(left, right)
    per = 32 // nxc
    for q in range(nxc):
        hist[q] = acc[q * per:(q + 1) * per, :]
    my_xc = x * CORES + core
    for ox, oc in xc_steps:
        o = ox * CORES + oc
        target = lax.rem(x + ox, nx) * CORES + lax.rem(core + oc, CORES)
        sent.append(send(hist.at[target], hist_x.at[o], hxs.at[o], hxr.at[o], peer(ox=ox, oc=oc)))

    p32 = pts[...].astype(F32)
    pts2[...] = (p32 * -2.0).astype(BF16)
    square = p32 * p32
    square_hi = square.astype(BF16)
    square_lo = (square - square_hi.astype(F32)).astype(BF16)
    ones = jnp.ones((16, D), BF16)
    norms = (contract_last(ones, square_hi) + contract_last(ones, square_lo))[0:1, :]

    def fold(block, masked):
        b32 = block.astype(F32)
        norm = jnp.sum(b32 * b32, axis=1, keepdims=True)
        if masked:
            place = lax.rem(lax.broadcasted_iota(I32, norm.shape, 0), blk)
            norm = jnp.where(place < rows, norm, BIG)
        for part in range(4):
            q = slice(part * 256, (part + 1) * 256)
            d = contract_last(block, pts2[q, :]) + norm
            least = jnp.min(d.reshape(d.shape[0] // 8, 8, 256), axis=0)
            nearest[:, q] = jnp.minimum(nearest[:, q], least)

    nearest[...] = jnp.full(nearest.shape, BIG, F32)

    def fold_centres(i, carry):
        fold(cen[pl.ds(pl.multiple_of(i * 512, 512), 512), :], False)
        return carry

    lax.fori_loop(0, cen.shape[0] // 512, fold_centres, 0)

    for o in near_first(nz):
        src = lax.rem(z + nz - o, nz)
        pltpu.make_async_remote_copy(
            src_ref=zbuf.at[src], dst_ref=zbuf.at[src], send_sem=zs.at[o], recv_sem=zr.at[o],
            device_id=peer(oz=o), device_id_type=MESH).wait_recv()
    column = jnp.concatenate([zbuf[i].astype(F32) for i in range(nz)], axis=0)
    crow = lax.broadcasted_iota(I32, column.shape, 0)
    clane = lax.broadcasted_iota(I32, column.shape, 1) & 127
    cdev = (clane * 43691) >> 18
    drop = ((crow & 7) >= slots) & ((crow >> 3) != cdev)
    column = jnp.where(drop, 0.0, column).astype(BF16)
    srow = lax.broadcasted_iota(I32, (blk, nz * 8), 0)
    scol = lax.broadcasted_iota(I32, (blk, nz * 8), 1)
    sdev = (srow * 43691) >> 18
    pick = (scol == sdev * 8 + (srow - sdev * slots)) & (srow < rows)
    pick = pick | ((srow == rows) & ((scol & 7) == slots))
    pick = pick | ((srow == rows + 1) & ((scol & 7) == slots + 1))
    packed = jnp.dot(jnp.where(pick, 1.0, 0.0).astype(BF16), column, preferred_element_type=F32)
    big[0, 0, 0] = packed.astype(BF16)

    def spread(o):
        for ox in near_first(nx):
            k = ox * ny + o
            sent.append(send(big.at[0, 0, o], big.at[0, ox, o], xs.at[k], xr.at[k], peer(ox=ox)))
        sent.append(send(big.at[0, 0, o], big.at[1, 0, o], cs.at[o], cr.at[o], peer(oc=1)))

    def arrive(dst, ssem, rsem, device):
        pltpu.make_async_remote_copy(
            src_ref=dst, dst_ref=dst, send_sem=ssem, recv_sem=rsem,
            device_id=device, device_id_type=MESH).wait_recv()

    for o in near_first(ny):
        sent.append(send(big.at[0, 0, 0], big.at[0, 0, o], ys.at[o], yr.at[o], peer(oy=o)))
    spread(0)

    total_h = hist[my_xc]
    for ox, oc in xc_steps:
        o = ox * CORES + oc
        arrive(hist_x.at[o], hxs.at[o], hxr.at[o], peer(ox=ox, oc=oc))
        total_h = total_h + hist_x[o]
    hist_z[0] = total_h
    for o in range(1, nz):
        sent.append(send(hist_z.at[0], hist_z.at[o], hzs.at[o], hzr.at[o], peer(oz=o)))

    for o in near_first(ny):
        arrive(big.at[0, 0, o], ys.at[o], yr.at[o], peer(oy=o))
        spread(o)

    def plane(c, ox):
        fold(big[c, ox].reshape(ny * blk, D), True)

    plane(0, 0)

    total_h = hist_z[0]
    for o in range(1, nz):
        arrive(hist_z.at[o], hzs.at[o], hzr.at[o], peer(oz=o))
        total_h = total_h + hist_z[o]
    hist_y[0] = total_h
    for o in range(1, ny):
        sent.append(send(hist_y.at[0], hist_y.at[o], hys.at[o], hyr.at[o], peer(oy=o)))

    for i, ox in enumerate(near_first(nx)):
        for o in [0] + near_first(ny):
            k = ox * ny + o
            arrive(big.at[0, ox, o], xs.at[k], xr.at[k], peer(ox=ox))
            sent.append(send(big.at[0, ox, o], big.at[1, ox, o], cs.at[k], cr.at[k], peer(oc=1)))
        plane(0, ox)
        if i == 0:
            total_h = hist_y[0]
            for o in range(1, ny):
                arrive(hist_y.at[o], hys.at[o], hyr.at[o], peer(oy=o))
                total_h = total_h + hist_y[o]
            counts[my_xc] = total_h
            for sx, sc in xc_steps:
                o = sx * CORES + sc
                sent.append(send(counts.at[my_xc], counts.at[my_xc], has.at[o], har.at[o],
                                 peer(ox=sx, oc=sc)))
    for ox in [0] + near_first(nx):
        for o in [0] + near_first(ny):
            k = ox * ny + o
            arrive(big.at[1, ox, o], cs.at[k], cr.at[k], peer(oc=1))
        plane(1, ox)

    best = jnp.maximum(jnp.min(nearest[...], axis=0, keepdims=True) + norms, 0.0)
    mass = jnp.sum(best, axis=1, keepdims=True)

    def stage(buf, ssem, rsem, steps, between):
        for o, device in steps:
            sent.append(send(buf.at[0], buf.at[o], ssem.at[o], rsem.at[o], device))
        between()
        result = buf[0]
        for o, device in steps:
            arrive(buf.at[o], ssem.at[o], rsem.at[o], device)
            result = result + buf[o]
        return result

    targets = row * (K_FINAL // (nx * ny * CORES)) + lax.broadcasted_iota(I32, (16, 128), 0)
    state = {}

    def product(member, table):
        parts = jnp.concatenate(split3(member), axis=0)
        out = jnp.dot(parts, table, preferred_element_type=F32)
        return out[0:16] + out[16:32] + out[32:48]

    def lloyd_centres():
        for ox, oc in xc_steps:
            o = ox * CORES + oc
            src = lax.rem(x + nx - ox, nx) * CORES + lax.rem(core + oc, CORES)
            arrive(counts.at[src], has.at[o], har.at[o], peer(ox=ox, oc=oc))
        weights = 1.0 + jnp.concatenate([counts[q] for q in range(nxc)], axis=0)
        pieces = []
        for t in range(16):
            hit = jnp.broadcast_to(owner_ref[t:t + 1, :], (16, 128)) == targets
            pieces.append(jnp.where(hit, jnp.broadcast_to(weights[t:t + 1, :], (16, 128)), 0.0))
        den = pieces[0]
        for t in range(1, 16):
            den = den + pieces[t]
        state["weights"] = weights
        state["den"] = den
        state["num"] = product(jnp.concatenate(pieces, axis=1), cen[...])

    def lloyd_slots(c):
        weights = state["weights"]
        num, den = state["num"], state["den"]
        for ox in range(nx):
            for o in range(ny):
                tail = big[c, ox, o, rows - 8:rows + 8, :].astype(F32)
                meta[0, o:o + 1, :] = tail[8:9, 0:128]
                meta[1, o:o + 1, :] = tail[8:9, 128:256]
                meta[2, o:o + 1, :] = tail[9:10, 0:128]
            code = (meta[0] + meta[1] * 256.0 + meta[2] * 65536.0).astype(I32) - 1
            valid = code >= 0
            owner = jnp.where(valid, code & 1023, -1)
            ident = jnp.where(valid, code >> 10, 0)
            high = ident >> 7
            low = ident & 127
            weight = jnp.zeros((ny, 128), F32)
            for h in range(16):
                table = jnp.broadcast_to(weights[16 + h:17 + h, :], (ny, 128))
                got = jnp.take_along_axis(table, low, axis=1)
                weight = jnp.where(high == h, got, weight)
            lanes = lax.broadcasted_iota(I32, (ny, 128), 1)
            owner = jnp.where(lanes < rows, owner, -1)
            for o in range(ny):
                hit = jnp.broadcast_to(owner[o:o + 1, :], (16, 128)) == targets
                member = jnp.where(hit, jnp.broadcast_to(weight[o:o + 1, :], (16, 128)), 0.0)
                den = den + member
                num = num + product(member[:, :blk], big[c, ox, o])
        state["num"], state["den"] = num, den

    tot_x[0] = jnp.broadcast_to(mass, (1, 128))
    xc = [(ox * CORES + oc, peer(ox=ox, oc=oc)) for ox, oc in xc_steps]
    tot_y[0] = stage(tot_x, txs, txr, xc, lloyd_centres)
    tot_z[0] = stage(tot_y, tys, tyr, [(o, peer(oy=o)) for o in range(1, ny)],
                     lambda: lloyd_slots(0))
    total = stage(tot_z, tzs, tzr, [(o, peer(oz=o)) for o in range(1, nz)],
                  lambda: lloyd_slots(1))
    den = jnp.sum(state["den"], axis=1, keepdims=True)
    final_ref[...] = state["num"] / den
    scaled = best * npts
    for b in range(8):
        cost_ref[b:b + 1, :] = scaled[:, b * 128:(b + 1) * 128] / total
    for copy in sent:
        copy.wait_send()


def shards(nx, ny, nz, points, centres, picks, assign_pts, cand_assign):
    nxc = nx * CORES
    blk = (nz * 2 * CAP + 2 + 15) // 16 * 16
    dma = pltpu.SemaphoreType.DMA
    per = 32 // nxc
    vmem = pl.BlockSpec(memory_space=pltpu.VMEM)
    hbm = pl.BlockSpec(memory_space=pl.ANY)
    scratch = [
        pltpu.VMEM(points.shape, BF16), pltpu.VMEM(points.shape, BF16),
        pltpu.VMEM(centres.shape, BF16), pltpu.VMEM((16, 128), I32),
        pltpu.VMEM((nz, 8, D), BF16), pltpu.VMEM((CORES, nx, ny, blk, D), BF16),
        pltpu.VMEM((8, 1024), F32), pltpu.VMEM((3, ny, 128), F32),
        pltpu.VMEM((nxc, per, 128), F32), pltpu.VMEM((nxc, per, 128), F32),
        pltpu.VMEM((nz, per, 128), F32), pltpu.VMEM((ny, per, 128), F32),
        pltpu.VMEM((nxc, per, 128), F32),
        pltpu.VMEM((nxc, 1, 128), F32), pltpu.VMEM((ny, 1, 128), F32),
        pltpu.VMEM((nz, 1, 128), F32), dma((2,)),
    ]
    for size in (nz, ny, nx * ny, nx * ny, nxc, nz, ny, nxc, nxc, ny, nz):
        scratch += [dma((size,)), dma((size,))]
    cost, final = pl.pallas_call(
        functools.partial(kernel, nx, ny, nz, float(1024 * nx * ny * CORES * nz)),
        out_shape=(jax.ShapeDtypeStruct((8, 128), F32), jax.ShapeDtypeStruct((16, D), F32)),
        in_specs=[vmem, vmem, vmem, hbm, hbm],
        out_specs=(vmem, vmem),
        scratch_shapes=scratch,
        compiler_params=pltpu.CompilerParams(
            collective_id=0, has_side_effects=True, vmem_limit_bytes=40 << 20),
    )(picks, cand_assign.reshape(32, 128), assign_pts.reshape(8, 128), points, centres)
    return cost.reshape(1024), final


def solution(mesh):
    nz = mesh.shape["col"]
    nx, ny = 4, mesh.shape["row"] // (4 * CORES)
    placed = (P(("row", "col"), None), P(), P(), P(("row", "col")), P())
    return jax.shard_map(
        functools.partial(shards, nx, ny, nz),
        mesh=mesh,
        in_specs=placed,
        out_specs=(P(("row", "col")), P("row", None)),
        check_vma=False,
    )
```

time: 316 us -> 67.4 us (0.21)
  blocking collectives: 242 us -> 0 us
  Pallas kernels: 0 us -> 60.1 us
  local copies, waits for them, and re-layouts: 53.9 us -> 5.56 us
  other arithmetic: 12.5 us -> 0 us
  matrix products: 5.48 us -> 0 us
    psum x2 -> x0, blocking collectives: 242 us -> none  [the longest x1 135 us: shards(): summed = lax.psum(picked.reshape(-1, feature_count), ('row', 'col'))]
    pallas_call x0 -> x1, Pallas kernels: none -> 60.1 us  [shards(): pl.pallas_call(functools.partial(kernel, nx, ny, nz, float(1024 * nx * ny...]
    gather x3 -> x0, local copies, waits for them, and re-layouts: 53.8 us -> none  [the longest x1 23 us: shards(): weights = jnp.where(keep_mask, 1.0 + counts[safe_ids], 0.0)]
    scatter-add x1 -> x0, other arithmetic: 6.05 us -> none  [shards(): jax.ops.segment_sum(jnp.ones((point_count,), jnp.float32), assign_pts, nu...]
    unnamed x10 -> x12, local copies, waits for them, and re-layouts: 0.03 us -> 5.56 us
    dot_general x9 -> x0, matrix products: 5.48 us -> none  [the longest x8 3.89 us: visit_block(): lax.dot_general(points, block_table, (((1,), (1,)), ((), ())), preferred_...]
where the time goes in v1:
time: 67.4 us; the launch traced here: 66.3 us
  Pallas kernels  60.1 us (89%)
  local copies, waits for them, and re-layouts  5.56 us (8%)
    pallas_call x1, Pallas kernels, shards(): pl.pallas_call(functools.partial(kernel, nx, ny, nz, float(1024 * nx * ny...  60.1 us
    unnamed x12, local copies, waits for them, and re-layouts  5.56 us

profile of v1, /device:TPU:1, one launch (start us, length us, event | category | flops | bytes accessed | tf_op | source)
XLA Modules:
  0.0 66.3 jit_solution(6346999432607148596)
XLA Ops:
  0.6 0.0 copy-start
  0.6 1.2 %copy-done = bf16[2048,256]{1,0:T(8,128)(2,1)S(1)} copy-done((bf16[2048,256]{1,0:T(8,128)(2,1)S(1)}, bf16[2048,256]{1,0:T(8,128)(2,1)}, u32[]{:S(2)}) %copy-start) | copy-done | bytes 1048600
  1.9 0.0 copy-start.1
  1.9 1.0 %copy-done.1 = bf16[1024,256]{1,0:T(8,128)(2,1)S(1)} copy-done((bf16[1024,256]{1,0:T(8,128)(2,1)S(1)}, bf16[1024,256]{1,0:T(8,128)(2,1)}, u32[]{:S(2)}) %copy-start.1) | copy-done | bytes 524312
  2.9 0.0 copy-start.2
  2.9 0.7 %copy-done.2 = s32[4096,1]{0,1:T(1,128)S(1)} copy-done((s32[4096,1]{0,1:T(1,128)S(1)}, s32[4096,1]{0,1:T(1,128)}, u32[]{:S(2)}) %copy-start.2) | copy-done | bytes 16408
  3.6 0.0 copy-start.3
  3.6 0.7 %copy-done.3 = s32[2,1024]{1,0:T(2,128)S(1)} copy-done((s32[2,1024]{1,0:T(2,128)S(1)}, s32[2,1024]{1,0:T(2,128)}, u32[]{:S(2)}) %copy-start.3) | copy-done | bytes 8216
  4.3 0.0 copy-start.4
  4.3 0.7 %copy-done.4 = s32[1024]{0:T(1024)S(1)} copy-done((s32[1024]{0:T(1024)S(1)}, s32[1024]{0:T(1024)}, u32[]{:S(2)}) %copy-start.4) | copy-done | bytes 4120
  5.0 60.1 %shard_map.68 = (f32[8,128]{1,0:T(8,128)S(1)}, f32[16,256]{1,0:T(8,128)S(1)}) custom-call(s32[2,1024]{1,0:T(2,128)S(1)} %copy-done.3, s32[32,128]{1,0:T(8,128)S(1)} %bitcast.3, s32[8,128]{1,0:T(8,128)S(1)} %bitcast.4, bf16[1024,256]{1,0:T(8,128)(2,1)S(1)} %copy-done.1, bf16[2048,256]{1,0:T(8,128)(2,1)S(1)} %copy-done), custom_call_target="tpu_custom_call" | custom-call | tf_op jit(solution)/shard_map/pallas_call | solution.py:370
  65.1 0.6 copy.9
  65.7 0.6 copy.10
Async XLA Ops:
  0.6 1.2 %copy-start = (bf16[2048,256]{1,0:T(8,128)(2,1)S(1)}, bf16[2048,256]{1,0:T(8,128)(2,1)}, u32[]{:S(2)}) copy-start(bf16[2048,256]{1,0:T(8,128)(2,1)} %centres_hbm.1) | copy-start | bytes 3145732
  1.9 1.0 %copy-start.1 = (bf16[1024,256]{1,0:T(8,128)(2,1)S(1)}, bf16[1024,256]{1,0:T(8,128)(2,1)}, u32[]{:S(2)}) copy-start(bf16[1024,256]{1,0:T(8,128)(2,1)} %points_hbm.1) | copy-start | bytes 1572868
  2.9 0.7 %copy-start.2 = (s32[4096,1]{0,1:T(1,128)S(1)}, s32[4096,1]{0,1:T(1,128)}, u32[]{:S(2)}) copy-start(s32[4096,1]{0,1:T(1,128)} %param.9) | copy-start | bytes 49156
  3.6 0.7 %copy-start.3 = (s32[2,1024]{1,0:T(2,128)S(1)}, s32[2,1024]{1,0:T(2,128)}, u32[]{:S(2)}) copy-start(s32[2,1024]{1,0:T(2,128)} %picks_ref.1) | copy-start | bytes 24580
  4.3 0.7 %copy-start.4 = (s32[1024]{0:T(1024)S(1)}, s32[1024]{0:T(1024)}, u32[]{:S(2)}) copy-start(s32[1024]{0:T(1024)} %param.8) | copy-start | bytes 12292

commit v2 on v1

--- a/solution.py
+++ b/solution.py
@@ -33,12 +33,12 @@
 
 
 def kernel(nx, ny, nz, npts,
-           picks_ref, owner_ref, assign_ref, points_hbm, centres_hbm,
+           picks_hbm, owner_hbm, assign_hbm, points_hbm, centres_hbm,
            cost_ref, final_ref,
-           pts, pts2, cen, picked, zbuf, big, nearest, meta,
+           picks_ref, owner_ref, assign_ref, pts, pts2, cen, picked, zbuf, big, nearest, meta,
            hist, hist_x, hist_z, hist_y, counts,
            tot_x, tot_y, tot_z, local_sem,
-           zs, zr, ys, yr, xs, xr, cs, cr,
+           zs, zr, bs, br, cs, cr,
            hxs, hxr, hzs, hzr, hys, hyr, has, har,
            txs, txr, tys, tyr, tzs, tzr):
     row = lax.axis_index("row")
@@ -65,10 +65,11 @@
         copy.start()
         return copy
 
-    load_points = pltpu.make_async_copy(points_hbm, pts, local_sem.at[0])
-    load_centres = pltpu.make_async_copy(centres_hbm, cen, local_sem.at[1])
-    load_points.start()
-    load_centres.start()
+    loads = [pltpu.make_async_copy(src, dst, local_sem.at[i]) for i, (src, dst) in enumerate(
+        [(picks_hbm, picks_ref), (owner_hbm, owner_ref), (points_hbm, pts),
+         (centres_hbm, cen), (assign_hbm, assign_ref)])]
+    for load in loads:
+        load.start()
 
     xc_steps = [(ox, oc) for ox in range(nx) for oc in range(CORES) if ox or oc]
     barrier = pltpu.get_barrier_semaphore()
@@ -77,6 +78,8 @@
     for other in peers:
         pl.semaphore_signal(barrier, inc=1, device_id=other, device_id_type=MESH)
 
+    loads[0].wait()
+    loads[1].wait()
     for r in range(2):
         for b in range(8):
             picked[r * 8 + b:r * 8 + b + 1, :] = picks_ref[r:r + 1, b * 128:(b + 1) * 128]
@@ -113,8 +116,9 @@
     digit_a = (code_row & 255).astype(F32)
     digit_b = ((code_row >> 8) & 255).astype(F32)
     digit_c = (code_row >> 16).astype(F32)
-    load_points.wait()
-    load_centres.wait()
+    loads[2].wait()
+    loads[3].wait()
+    loads[4].wait()
     mine = jnp.dot(choose16, pts[...], preferred_element_type=F32)[:8, :]
     slot_col = lax.broadcasted_iota(I32, (8, D), 0)
     filled = jnp.zeros((8, D), I32)
@@ -131,7 +135,6 @@
     pl.semaphore_wait(barrier, len(peers))
 
     sent = []
-    zcopies = {}
     for o in near_first(nz)[::-1]:
         copy = send(zbuf.at[z], zbuf.at[z], zs.at[o], zr.at[o], peer(oz=o))
         sent.append(copy)
@@ -201,20 +204,45 @@
     packed = jnp.dot(jnp.where(pick, 1.0, 0.0).astype(BF16), column, preferred_element_type=F32)
     big[0, 0, 0] = packed.astype(BF16)
 
-    def spread(o):
-        for ox in near_first(nx):
-            k = ox * ny + o
-            sent.append(send(big.at[0, 0, o], big.at[0, ox, o], xs.at[k], xr.at[k], peer(ox=ox)))
-        sent.append(send(big.at[0, 0, o], big.at[1, 0, o], cs.at[o], cr.at[o], peer(oc=1)))
-
     def arrive(dst, ssem, rsem, device):
         pltpu.make_async_remote_copy(
             src_ref=dst, dst_ref=dst, send_sem=ssem, recv_sem=rsem,
             device_id=device, device_id_type=MESH).wait_recv()
 
-    for o in near_first(ny):
-        sent.append(send(big.at[0, 0, 0], big.at[0, 0, o], ys.at[o], yr.at[o], peer(oy=o)))
-    spread(0)
+    def forward(o, ox, to_o, to_ox, device):
+        k = to_o * nx + to_ox
+        sent.append(send(big.at[0, o, ox], big.at[0, to_o, to_ox], bs.at[k], br.at[k], device))
+
+    def swap(o, ox):
+        k = o * nx + ox
+        sent.append(send(big.at[0, o, ox], big.at[1, o, ox], cs.at[k], cr.at[k], peer(oc=1)))
+
+    def sideways(o, ox):
+        if o == 0 or o == 2:
+            forward(o, ox, o + 1, ox, peer(oy=1))
+        if o == 0 or o == ny - 2:
+            forward(o, ox, (o + ny - 1) % ny, ox, peer(oy=ny - 1))
+
+    def landed(o, ox):
+        k = o * nx + ox
+        arrive(big.at[0, o, ox], bs.at[k], br.at[k], peer(oy=1))
+
+    def swapped(o):
+        for ox in range(nx):
+            k = o * nx + ox
+            arrive(big.at[1, o, ox], cs.at[k], cr.at[k], peer(oc=1))
+
+    def unit(c, o):
+        fold(big[c, o].reshape(nx * blk, D), True)
+
+    xs = near_first(nx)
+    far_y = (2, ny - 2, 4)
+    for o in far_y:
+        forward(0, 0, o, 0, peer(oy=o))
+    for ox in xs:
+        forward(0, 0, 0, ox, peer(ox=ox))
+    sideways(0, 0)
+    swap(0, 0)
 
     total_h = hist[my_xc]
     for ox, oc in xc_steps:
@@ -225,14 +253,20 @@
     for o in range(1, nz):
         sent.append(send(hist_z.at[0], hist_z.at[o], hzs.at[o], hzr.at[o], peer(oz=o)))
 
-    for o in near_first(ny):
-        arrive(big.at[0, 0, o], ys.at[o], yr.at[o], peer(oy=o))
-        spread(o)
-
-    def plane(c, ox):
-        fold(big[c, ox].reshape(ny * blk, D), True)
-
-    plane(0, 0)
+    for o in (1, ny - 1):
+        landed(o, 0)
+        swap(o, 0)
+    for ox in xs:
+        landed(0, ox)
+        sideways(0, ox)
+        swap(0, ox)
+    for o in far_y:
+        landed(o, 0)
+        for ox in xs:
+            forward(o, 0, o, ox, peer(ox=ox))
+        sideways(o, 0)
+        swap(o, 0)
+    unit(0, 0)
 
     total_h = hist_z[0]
     for o in range(1, nz):
@@ -242,27 +276,54 @@
     for o in range(1, ny):
         sent.append(send(hist_y.at[0], hist_y.at[o], hys.at[o], hyr.at[o], peer(oy=o)))
 
-    for i, ox in enumerate(near_first(nx)):
-        for o in [0] + near_first(ny):
-            k = ox * ny + o
-            arrive(big.at[0, ox, o], xs.at[k], xr.at[k], peer(ox=ox))
-            sent.append(send(big.at[0, ox, o], big.at[1, ox, o], cs.at[k], cr.at[k], peer(oc=1)))
-        plane(0, ox)
-        if i == 0:
-            total_h = hist_y[0]
-            for o in range(1, ny):
-                arrive(hist_y.at[o], hys.at[o], hyr.at[o], peer(oy=o))
-                total_h = total_h + hist_y[o]
-            counts[my_xc] = total_h
-            for sx, sc in xc_steps:
-                o = sx * CORES + sc
-                sent.append(send(counts.at[my_xc], counts.at[my_xc], has.at[o], har.at[o],
-                                 peer(ox=sx, oc=sc)))
-    for ox in [0] + near_first(nx):
-        for o in [0] + near_first(ny):
-            k = ox * ny + o
-            arrive(big.at[1, ox, o], cs.at[k], cr.at[k], peer(oc=1))
-        plane(1, ox)
+    for o in (1, ny - 1):
+        for ox in xs:
+            landed(o, ox)
+            swap(o, ox)
+    swapped(0)
+    unit(1, 0)
+    for o in (3, ny - 3):
+        landed(o, 0)
+        swap(o, 0)
+    unit(0, 1)
+    for o in far_y[:2]:
+        for ox in xs:
+            landed(o, ox)
+            sideways(o, ox)
+            swap(o, ox)
+    unit(0, ny - 1)
+    for ox in xs:
+        landed(4, ox)
+        swap(4, ox)
+    unit(0, 2)
+    swapped(1)
+    unit(1, 1)
+
+    total_h = hist_y[0]
+    for o in range(1, ny):
+        arrive(hist_y.at[o], hys.at[o], hyr.at[o], peer(oy=o))
+        total_h = total_h + hist_y[o]
+    counts[my_xc] = total_h
+    for ox, oc in xc_steps:
+        o = ox * CORES + oc
+        sent.append(send(counts.at[my_xc], counts.at[my_xc], has.at[o], har.at[o], peer(ox=ox, oc=oc)))
+
+    unit(0, ny - 2)
+    swapped(ny - 1)
+    unit(1, ny - 1)
+    unit(0, 4)
+    for o in (3, ny - 3):
+        for ox in xs:
+            landed(o, ox)
+            swap(o, ox)
+    for o in far_y:
+        swapped(o)
+        unit(1, o)
+    for o in (3, ny - 3):
+        unit(0, o)
+    for o in (3, ny - 3):
+        swapped(o)
+        unit(1, o)
 
     best = jnp.maximum(jnp.min(nearest[...], axis=0, keepdims=True) + norms, 0.0)
     mass = jnp.sum(best, axis=1, keepdims=True)
@@ -307,7 +368,7 @@
         num, den = state["num"], state["den"]
         for ox in range(nx):
             for o in range(ny):
-                tail = big[c, ox, o, rows - 8:rows + 8, :].astype(F32)
+                tail = big[c, o, ox, rows - 8:rows + 8, :].astype(F32)
                 meta[0, o:o + 1, :] = tail[8:9, 0:128]
                 meta[1, o:o + 1, :] = tail[8:9, 128:256]
                 meta[2, o:o + 1, :] = tail[9:10, 0:128]
@@ -328,7 +389,7 @@
                 hit = jnp.broadcast_to(owner[o:o + 1, :], (16, 128)) == targets
                 member = jnp.where(hit, jnp.broadcast_to(weight[o:o + 1, :], (16, 128)), 0.0)
                 den = den + member
-                num = num + product(member[:, :blk], big[c, ox, o])
+                num = num + product(member[:, :blk], big[c, o, ox])
         state["num"], state["den"] = num, den
 
     tot_x[0] = jnp.broadcast_to(mass, (1, 128))
@@ -353,28 +414,29 @@
     dma = pltpu.SemaphoreType.DMA
     per = 32 // nxc
     vmem = pl.BlockSpec(memory_space=pltpu.VMEM)
-    hbm = pl.BlockSpec(memory_space=pl.ANY)
+    hbm = pl.BlockSpec(memory_space=pltpu.MemorySpace.HBM)
     scratch = [
+        pltpu.VMEM(picks.shape, I32), pltpu.VMEM((32, 128), I32), pltpu.VMEM((8, 128), I32),
         pltpu.VMEM(points.shape, BF16), pltpu.VMEM(points.shape, BF16),
         pltpu.VMEM(centres.shape, BF16), pltpu.VMEM((16, 128), I32),
-        pltpu.VMEM((nz, 8, D), BF16), pltpu.VMEM((CORES, nx, ny, blk, D), BF16),
+        pltpu.VMEM((nz, 8, D), BF16), pltpu.VMEM((CORES, ny, nx, blk, D), BF16),
         pltpu.VMEM((8, 1024), F32), pltpu.VMEM((3, ny, 128), F32),
         pltpu.VMEM((nxc, per, 128), F32), pltpu.VMEM((nxc, per, 128), F32),
         pltpu.VMEM((nz, per, 128), F32), pltpu.VMEM((ny, per, 128), F32),
         pltpu.VMEM((nxc, per, 128), F32),
         pltpu.VMEM((nxc, 1, 128), F32), pltpu.VMEM((ny, 1, 128), F32),
-        pltpu.VMEM((nz, 1, 128), F32), dma((2,)),
+        pltpu.VMEM((nz, 1, 128), F32), dma((5,)),
     ]
-    for size in (nz, ny, nx * ny, nx * ny, nxc, nz, ny, nxc, nxc, ny, nz):
+    for size in (nz, nx * ny, nx * ny, nxc, nz, ny, nxc, nxc, ny, nz):
         scratch += [dma((size,)), dma((size,))]
     cost, final = pl.pallas_call(
         functools.partial(kernel, nx, ny, nz, float(1024 * nx * ny * CORES * nz)),
         out_shape=(jax.ShapeDtypeStruct((8, 128), F32), jax.ShapeDtypeStruct((16, D), F32)),
-        in_specs=[vmem, vmem, vmem, hbm, hbm],
+        in_specs=[hbm] * 5,
         out_specs=(vmem, vmem),
         scratch_shapes=scratch,
         compiler_params=pltpu.CompilerParams(
-            collective_id=0, has_side_effects=True, vmem_limit_bytes=40 << 20),
+            collective_id=0, has_side_effects=True, vmem_limit_bytes=60 << 20),
     )(picks, cand_assign.reshape(32, 128), assign_pts.reshape(8, 128), points, centres)
     return cost.reshape(1024), final
 

time: 67.4 us -> 62.2 us (0.923)
  local copies, waits for them, and re-layouts: 5.56 us -> 2.59 us
  Pallas kernels: 60.1 us -> 58.2 us
    unnamed x12 -> x4, local copies, waits for them, and re-layouts: 5.56 us -> 2.59 us
    pallas_call x1, Pallas kernels: 60.1 us -> 58.2 us  [shards(): pl.pallas_call(functools.partial(kernel, nx, ny, nz, float(1024 * nx * ny...]
where the time goes in v2:
time: 62.2 us; the launch traced here: 61.4 us
  Pallas kernels  58.2 us (94%)
  local copies, waits for them, and re-layouts  2.59 us (4%)
  between operations  0.65 us (1%)
    pallas_call x1, Pallas kernels, shards(): pl.pallas_call(functools.partial(kernel, nx, ny, nz, float(1024 * nx * ny...  58.2 us
    unnamed x4, local copies, waits for them, and re-layouts  2.59 us

profile of v2, /device:TPU:1, one launch (start us, length us, event | category | flops | bytes accessed | tf_op | source)
XLA Modules:
  0.0 61.4 jit_solution(6833688160435909538)
XLA Ops:
  0.6 58.2 %shard_map.68 = (f32[8,128]{1,0:T(8,128)}, f32[16,256]{1,0:T(8,128)}) custom-call(s32[2,1024]{1,0:T(2,128)} %picks_hbm.1, s32[32,128]{1,0:T(8,128)} %bitcast.3, s32[8,128]{1,0:T(8,128)} %bitcast.4, bf16[1024,256]{1,0:T(8,128)(2,1)} %points_hbm.1, bf16[2048,256]{1,0:T(8,128)(2,1)} %centres_hbm.1), custom_call_target="tpu_custom_call" | custom-call | tf_op jit(solution)/shard_map/pallas_call | solution.py:432
  58.8 0.0 copy-start
  58.8 0.7 %copy-done = f32[8,128]{1,0:T(8,128)S(1)} copy-done((f32[8,128]{1,0:T(8,128)S(1)}, f32[8,128]{1,0:T(8,128)}, u32[]{:S(2)}) %copy-start) | copy-done | bytes 4120
  59.5 0.6 copy.9
  60.1 1.3 %copy.10 = f32[16,256]{1,0:T(8,128)} copy(f32[16,256]{1,0:T(8,128)} %get-tuple-element.9) | data formatting | bytes 32768
Async XLA Ops:
  58.8 0.7 %copy-start = (f32[8,128]{1,0:T(8,128)S(1)}, f32[8,128]{1,0:T(8,128)}, u32[]{:S(2)}) copy-start(f32[8,128]{1,0:T(8,128)} %get-tuple-element.4) | copy-start | bytes 12292

commit v3 on v2

--- a/solution.py
+++ b/solution.py
@@ -37,10 +37,7 @@
            cost_ref, final_ref,
            picks_ref, owner_ref, assign_ref, pts, pts2, cen, picked, zbuf, big, nearest, meta,
            hist, hist_x, hist_z, hist_y, counts,
-           tot_x, tot_y, tot_z, local_sem,
-           zs, zr, bs, br, cs, cr,
-           hxs, hxr, hzs, hzr, hys, hyr, has, har,
-           txs, txr, tys, tyr, tzs, tzr):
+           tot_x, tot_y, tot_z, local_sem, ssem, rsem, block_sem, swap_sem):
     row = lax.axis_index("row")
     z = lax.axis_index("col")
     core = lax.rem(row, CORES)
@@ -58,12 +55,24 @@
         pc = lax.rem(core + oc, CORES)
         return ((px * ny + py) * CORES + pc, lax.rem(z + oz, nz))
 
-    def send(src, dst, ssem, rsem, device):
-        copy = pltpu.make_async_remote_copy(
-            src_ref=src, dst_ref=dst, send_sem=ssem, recv_sem=rsem,
-            device_id=device, device_id_type=MESH)
-        copy.start()
-        return copy
+    def send(src, dst, out_sem, in_sem, device):
+        pltpu.make_async_remote_copy(
+            src_ref=src, dst_ref=dst, send_sem=out_sem, recv_sem=in_sem,
+            device_id=device, device_id_type=MESH).start()
+
+    def waiter(ref, sem):
+        return pltpu.make_async_remote_copy(
+            src_ref=ref, dst_ref=ref, send_sem=sem, recv_sem=sem,
+            device_id=peer(oz=1), device_id_type=MESH)
+
+    def arrive(ref, sem):
+        waiter(ref, sem).wait_recv()
+
+    def drain(ref, sem):
+        waiter(ref, sem).wait_send()
+
+    def others(ref, size):
+        return ref.at[pl.ds(0, size - 1)]
 
     loads = [pltpu.make_async_copy(src, dst, local_sem.at[i]) for i, (src, dst) in enumerate(
         [(picks_hbm, picks_ref), (owner_hbm, owner_ref), (points_hbm, pts),
@@ -134,10 +143,8 @@
 
     pl.semaphore_wait(barrier, len(peers))
 
-    sent = []
     for o in near_first(nz)[::-1]:
-        copy = send(zbuf.at[z], zbuf.at[z], zs.at[o], zr.at[o], peer(oz=o))
-        sent.append(copy)
+        send(zbuf.at[z], zbuf.at[z], ssem.at[0], rsem.at[0], peer(oz=o))
 
     acc = jnp.zeros((32, 128), F32)
     hi_iota = lax.broadcasted_iota(I32, (32, 128), 0)
@@ -154,7 +161,7 @@
     for ox, oc in xc_steps:
         o = ox * CORES + oc
         target = lax.rem(x + ox, nx) * CORES + lax.rem(core + oc, CORES)
-        sent.append(send(hist.at[target], hist_x.at[o], hxs.at[o], hxr.at[o], peer(ox=ox, oc=oc)))
+        send(hist.at[target], hist_x.at[o], ssem.at[1], rsem.at[1], peer(ox=ox, oc=oc))
 
     p32 = pts[...].astype(F32)
     pts2[...] = (p32 * -2.0).astype(BF16)
@@ -184,11 +191,7 @@
 
     lax.fori_loop(0, cen.shape[0] // 512, fold_centres, 0)
 
-    for o in near_first(nz):
-        src = lax.rem(z + nz - o, nz)
-        pltpu.make_async_remote_copy(
-            src_ref=zbuf.at[src], dst_ref=zbuf.at[src], send_sem=zs.at[o], recv_sem=zr.at[o],
-            device_id=peer(oz=o), device_id_type=MESH).wait_recv()
+    arrive(others(zbuf, nz), rsem.at[0])
     column = jnp.concatenate([zbuf[i].astype(F32) for i in range(nz)], axis=0)
     crow = lax.broadcasted_iota(I32, column.shape, 0)
     clane = lax.broadcasted_iota(I32, column.shape, 1) & 127
@@ -204,138 +207,147 @@
     packed = jnp.dot(jnp.where(pick, 1.0, 0.0).astype(BF16), column, preferred_element_type=F32)
     big[0, 0, 0] = packed.astype(BF16)
 
-    def arrive(dst, ssem, rsem, device):
-        pltpu.make_async_remote_copy(
-            src_ref=dst, dst_ref=dst, send_sem=ssem, recv_sem=rsem,
-            device_id=device, device_id_type=MESH).wait_recv()
-
-    def forward(o, ox, to_o, to_ox, device):
-        k = to_o * nx + to_ox
-        sent.append(send(big.at[0, o, ox], big.at[0, to_o, to_ox], bs.at[k], br.at[k], device))
+    parity = lax.rem(z, 2)
+    steps = (0, 3, 1, 2)
+    xs = near_first(nx)
+
+    def mine_of(i):
+        return 2 * i + parity
+
+    def theirs_of(i):
+        return 2 * i + 1 - parity
+
+    def slot(o, ox):
+        return block_sem.at[o * nx + ox]
+
+    def forward(o, ox, to_o, to_ox, out_sem, device):
+        send(big.at[0, o, ox], big.at[0, to_o, to_ox], ssem.at[out_sem], slot(to_o, to_ox), device)
 
     def swap(o, ox):
-        k = o * nx + ox
-        sent.append(send(big.at[0, o, ox], big.at[1, o, ox], cs.at[k], cr.at[k], peer(oc=1)))
-
-    def sideways(o, ox):
-        if o == 0 or o == 2:
-            forward(o, ox, o + 1, ox, peer(oy=1))
-        if o == 0 or o == ny - 2:
-            forward(o, ox, (o + ny - 1) % ny, ox, peer(oy=ny - 1))
+        send(big.at[0, o, ox], big.at[1, o, ox], ssem.at[8], swap_sem.at[o], peer(oc=1))
+
+    def upright(i, ox, out_sem):
+        o = mine_of(i)
+        forward(o, ox, o, ox, out_sem, peer(oz=1 if i < 2 else nz - 1))
 
     def landed(o, ox):
-        k = o * nx + ox
-        arrive(big.at[0, o, ox], bs.at[k], br.at[k], peer(oy=1))
-
-    def swapped(o):
-        for ox in range(nx):
-            k = o * nx + ox
-            arrive(big.at[1, o, ox], cs.at[k], cr.at[k], peer(oc=1))
+        arrive(big.at[0, o, ox], slot(o, ox))
+
+    def across(i):
+        o = mine_of(i)
+        for ox in xs:
+            forward(o, 0, o, ox, 11, peer(ox=ox))
+
+    def from_x(i):
+        for ox in xs:
+            landed(mine_of(i), ox)
+            upright(i, ox, 12 if i else 13)
+            swap(mine_of(i), ox)
+
+    def from_z(i):
+        o = theirs_of(i)
+        if i:
+            landed(o, 0)
+            swap(o, 0)
+        else:
+            @pl.when(parity == 0)
+            def _():
+                landed(o, 0)
+                swap(o, 0)
+        for ox in xs:
+            landed(o, ox)
+            swap(o, ox)
 
     def unit(c, o):
         fold(big[c, o].reshape(nx * blk, D), True)
 
-    xs = near_first(nx)
-    far_y = (2, ny - 2, 4)
-    for o in far_y:
-        forward(0, 0, o, 0, peer(oy=o))
-    for ox in xs:
-        forward(0, 0, 0, ox, peer(ox=ox))
-    sideways(0, 0)
+    def swapped(o):
+        arrive(big.at[1, o], swap_sem.at[o])
+        unit(1, o)
+
+    for i in (2, 1, 3):
+        forward(0, 0, mine_of(i), 0, 9, peer(oy=mine_of(i)))
+
+    @pl.when(parity == 1)
+    def _():
+        forward(0, 0, 1, 0, 10, peer(oy=1))
+
     swap(0, 0)
 
+    arrive(others(hist_x, nxc), rsem.at[1])
     total_h = hist[my_xc]
-    for ox, oc in xc_steps:
-        o = ox * CORES + oc
-        arrive(hist_x.at[o], hxs.at[o], hxr.at[o], peer(ox=ox, oc=oc))
+    for o in range(1, nxc):
         total_h = total_h + hist_x[o]
     hist_z[0] = total_h
+
+    @pl.when(parity == 1)
+    def _():
+        landed(1, 0)
+        upright(0, 0, 14)
+        swap(1, 0)
+
+    across(0)
     for o in range(1, nz):
-        sent.append(send(hist_z.at[0], hist_z.at[o], hzs.at[o], hzr.at[o], peer(oz=o)))
-
-    for o in (1, ny - 1):
-        landed(o, 0)
-        swap(o, 0)
-    for ox in xs:
-        landed(0, ox)
-        sideways(0, ox)
-        swap(0, ox)
-    for o in far_y:
-        landed(o, 0)
-        for ox in xs:
-            forward(o, 0, o, ox, peer(ox=ox))
-        sideways(o, 0)
-        swap(o, 0)
-    unit(0, 0)
-
+        send(hist_z.at[0], hist_z.at[o], ssem.at[2], rsem.at[2], peer(oz=o))
+    for i in steps[1:]:
+        landed(mine_of(i), 0)
+        across(i)
+        upright(i, 0, 12)
+        swap(mine_of(i), 0)
+    from_x(0)
+    unit(0, mine_of(0))
+
+    arrive(others(hist_z, nz), rsem.at[2])
     total_h = hist_z[0]
     for o in range(1, nz):
-        arrive(hist_z.at[o], hzs.at[o], hzr.at[o], peer(oz=o))
         total_h = total_h + hist_z[o]
     hist_y[0] = total_h
     for o in range(1, ny):
-        sent.append(send(hist_y.at[0], hist_y.at[o], hys.at[o], hyr.at[o], peer(oy=o)))
-
-    for o in (1, ny - 1):
-        for ox in xs:
-            landed(o, ox)
-            swap(o, ox)
-    swapped(0)
-    unit(1, 0)
-    for o in (3, ny - 3):
-        landed(o, 0)
-        swap(o, 0)
-    unit(0, 1)
-    for o in far_y[:2]:
-        for ox in xs:
-            landed(o, ox)
-            sideways(o, ox)
-            swap(o, ox)
-    unit(0, ny - 1)
-    for ox in xs:
-        landed(4, ox)
-        swap(4, ox)
-    unit(0, 2)
-    swapped(1)
-    unit(1, 1)
-
+        send(hist_y.at[0], hist_y.at[o], ssem.at[3], rsem.at[3], peer(oy=o))
+
+    from_x(3)
+    unit(0, mine_of(3))
+    from_z(0)
+    swapped(mine_of(0))
+    from_x(1)
+    unit(0, mine_of(1))
+    from_z(3)
+    unit(0, theirs_of(0))
+    swapped(mine_of(3))
+
+    arrive(others(hist_y, ny), rsem.at[3])
     total_h = hist_y[0]
     for o in range(1, ny):
-        arrive(hist_y.at[o], hys.at[o], hyr.at[o], peer(oy=o))
         total_h = total_h + hist_y[o]
     counts[my_xc] = total_h
     for ox, oc in xc_steps:
-        o = ox * CORES + oc
-        sent.append(send(counts.at[my_xc], counts.at[my_xc], has.at[o], har.at[o], peer(ox=ox, oc=oc)))
-
-    unit(0, ny - 2)
-    swapped(ny - 1)
-    unit(1, ny - 1)
-    unit(0, 4)
-    for o in (3, ny - 3):
-        for ox in xs:
-            landed(o, ox)
-            swap(o, ox)
-    for o in far_y:
-        swapped(o)
-        unit(1, o)
-    for o in (3, ny - 3):
-        unit(0, o)
-    for o in (3, ny - 3):
-        swapped(o)
-        unit(1, o)
+        send(counts.at[my_xc], counts.at[my_xc], ssem.at[4], rsem.at[4], peer(ox=ox, oc=oc))
+
+    from_x(2)
+    unit(0, mine_of(2))
+    from_z(1)
+    unit(0, theirs_of(3))
+    swapped(theirs_of(0))
+    swapped(mine_of(1))
+    from_z(2)
+    unit(0, theirs_of(1))
+    swapped(theirs_of(3))
+    swapped(mine_of(2))
+    unit(0, theirs_of(2))
+    swapped(theirs_of(1))
+    swapped(theirs_of(2))
 
     best = jnp.maximum(jnp.min(nearest[...], axis=0, keepdims=True) + norms, 0.0)
     mass = jnp.sum(best, axis=1, keepdims=True)
 
-    def stage(buf, ssem, rsem, steps, between):
-        for o, device in steps:
-            sent.append(send(buf.at[0], buf.at[o], ssem.at[o], rsem.at[o], device))
+    def stage(buf, sem, devices, between):
+        for o, device in enumerate(devices):
+            send(buf.at[0], buf.at[o + 1], ssem.at[sem], rsem.at[sem], device)
         between()
+        arrive(others(buf, len(devices) + 1), rsem.at[sem])
         result = buf[0]
-        for o, device in steps:
-            arrive(buf.at[o], ssem.at[o], rsem.at[o], device)
-            result = result + buf[o]
+        for o in range(len(devices)):
+            result = result + buf[o + 1]
         return result
 
     targets = row * (K_FINAL // (nx * ny * CORES)) + lax.broadcasted_iota(I32, (16, 128), 0)
@@ -347,10 +359,7 @@
         return out[0:16] + out[16:32] + out[32:48]
 
     def lloyd_centres():
-        for ox, oc in xc_steps:
-            o = ox * CORES + oc
-            src = lax.rem(x + nx - ox, nx) * CORES + lax.rem(core + oc, CORES)
-            arrive(counts.at[src], has.at[o], har.at[o], peer(ox=ox, oc=oc))
+        arrive(others(counts, nxc), rsem.at[4])
         weights = 1.0 + jnp.concatenate([counts[q] for q in range(nxc)], axis=0)
         pieces = []
         for t in range(16):
@@ -393,19 +402,32 @@
         state["num"], state["den"] = num, den
 
     tot_x[0] = jnp.broadcast_to(mass, (1, 128))
-    xc = [(ox * CORES + oc, peer(ox=ox, oc=oc)) for ox, oc in xc_steps]
-    tot_y[0] = stage(tot_x, txs, txr, xc, lloyd_centres)
-    tot_z[0] = stage(tot_y, tys, tyr, [(o, peer(oy=o)) for o in range(1, ny)],
-                     lambda: lloyd_slots(0))
-    total = stage(tot_z, tzs, tzr, [(o, peer(oz=o)) for o in range(1, nz)],
-                  lambda: lloyd_slots(1))
+    tot_y[0] = stage(tot_x, 5, [peer(ox=ox, oc=oc) for ox, oc in xc_steps], lloyd_centres)
+    tot_z[0] = stage(tot_y, 6, [peer(oy=o) for o in range(1, ny)], lambda: lloyd_slots(0))
+    total = stage(tot_z, 7, [peer(oz=o) for o in range(1, nz)], lambda: lloyd_slots(1))
     den = jnp.sum(state["den"], axis=1, keepdims=True)
     final_ref[...] = state["num"] / den
     scaled = best * npts
     for b in range(8):
         cost_ref[b:b + 1, :] = scaled[:, b * 128:(b + 1) * 128] / total
-    for copy in sent:
-        copy.wait_send()
+    drain(others(zbuf, nz), ssem.at[0])
+    drain(others(hist_x, nxc), ssem.at[1])
+    drain(others(hist_z, nz), ssem.at[2])
+    drain(others(hist_y, ny), ssem.at[3])
+    drain(others(counts, nxc), ssem.at[4])
+    drain(others(tot_x, nxc), ssem.at[5])
+    drain(others(tot_y, ny), ssem.at[6])
+    drain(others(tot_z, nz), ssem.at[7])
+    drain(big.at[1], ssem.at[8])
+    drain(big.at[0, 0, pl.ds(0, 3)], ssem.at[9])
+    drain(big.at[0, pl.ds(0, nx - 1)], ssem.at[11])
+    drain(big.at[0, pl.ds(0, 3)], ssem.at[12])
+    drain(big.at[0, 0, pl.ds(0, nx - 1)], ssem.at[13])
+
+    @pl.when(parity == 1)
+    def _():
+        drain(big.at[0, 0, 0], ssem.at[10])
+        drain(big.at[0, 0, 0], ssem.at[14])
 
 
 def shards(nx, ny, nz, points, centres, picks, assign_pts, cand_assign):
@@ -427,8 +449,7 @@
         pltpu.VMEM((nxc, 1, 128), F32), pltpu.VMEM((ny, 1, 128), F32),
         pltpu.VMEM((nz, 1, 128), F32), dma((5,)),
     ]
-    for size in (nz, nx * ny, nx * ny, nxc, nz, ny, nxc, nxc, ny, nz):
-        scratch += [dma((size,)), dma((size,))]
+    scratch += [dma((15,)), dma((8,)), dma((nx * ny,)), dma((ny,))]
     cost, final = pl.pallas_call(
         functools.partial(kernel, nx, ny, nz, float(1024 * nx * ny * CORES * nz)),
         out_shape=(jax.ShapeDtypeStruct((8, 128), F32), jax.ShapeDtypeStruct((16, D), F32)),

time: 62.2 us -> 64.9 us (1.043)
  Pallas kernels: 58.2 us -> 60.6 us
    pallas_call x1, Pallas kernels: 58.2 us -> 60.6 us  [shards(): pl.pallas_call(functools.partial(kernel, nx, ny, nz, float(1024 * nx * ny...]
where the time goes in v3:
time: 64.9 us; the launch traced here: 63.8 us
  Pallas kernels  60.6 us (93%)
  local copies, waits for them, and re-layouts  2.59 us (4%)
  between operations  0.65 us (1%)
    pallas_call x1, Pallas kernels, shards(): pl.pallas_call(functools.partial(kernel, nx, ny, nz, float(1024 * nx * ny...  60.6 us
    unnamed x4, local copies, waits for them, and re-layouts  2.59 us

profile of v3, /device:TPU:1, one launch (start us, length us, event | category | flops | bytes accessed | tf_op | source)
XLA Modules:
  0.0 63.8 jit_solution(10184214848418144258)
XLA Ops:
  0.6 60.6 %shard_map.68 = (f32[8,128]{1,0:T(8,128)}, f32[16,256]{1,0:T(8,128)}) custom-call(s32[2,1024]{1,0:T(2,128)} %picks_hbm.1, s32[32,128]{1,0:T(8,128)} %bitcast.3, s32[8,128]{1,0:T(8,128)} %bitcast.4, bf16[1024,256]{1,0:T(8,128)(2,1)} %points_hbm.1, bf16[2048,256]{1,0:T(8,128)(2,1)} %centres_hbm.1), custom_call_target="tpu_custom_call" | custom-call | tf_op jit(solution)/shard_map/pallas_call | solution.py:453
  61.2 0.0 copy-start
  61.2 0.7 %copy-done = f32[8,128]{1,0:T(8,128)S(1)} copy-done((f32[8,128]{1,0:T(8,128)S(1)}, f32[8,128]{1,0:T(8,128)}, u32[]{:S(2)}) %copy-start) | copy-done | bytes 4120
  61.9 0.6 copy.9
  62.5 1.3 %copy.10 = f32[16,256]{1,0:T(8,128)} copy(f32[16,256]{1,0:T(8,128)} %get-tuple-element.9) | data formatting | bytes 32768
Async XLA Ops:
  61.2 0.7 %copy-start = (f32[8,128]{1,0:T(8,128)S(1)}, f32[8,128]{1,0:T(8,128)}, u32[]{:S(2)}) copy-start(f32[8,128]{1,0:T(8,128)} %get-tuple-element.4) | copy-start | bytes 12292

commit v4 on v3

--- a/solution.py
+++ b/solution.py
@@ -207,15 +207,8 @@
     packed = jnp.dot(jnp.where(pick, 1.0, 0.0).astype(BF16), column, preferred_element_type=F32)
     big[0, 0, 0] = packed.astype(BF16)
 
-    parity = lax.rem(z, 2)
-    steps = (0, 3, 1, 2)
     xs = near_first(nx)
-
-    def mine_of(i):
-        return 2 * i + parity
-
-    def theirs_of(i):
-        return 2 * i + 1 - parity
+    far_y = (2, ny - 2, 4)
 
     def slot(o, ox):
         return block_sem.at[o * nx + ox]
@@ -226,37 +219,18 @@
     def swap(o, ox):
         send(big.at[0, o, ox], big.at[1, o, ox], ssem.at[8], swap_sem.at[o], peer(oc=1))
 
-    def upright(i, ox, out_sem):
-        o = mine_of(i)
-        forward(o, ox, o, ox, out_sem, peer(oz=1 if i < 2 else nz - 1))
+    def sideways(o, ox):
+        if o == 0 or o == 2:
+            forward(o, ox, o + 1, ox, 11, peer(oy=1))
+        if o == 0 or o == ny - 2:
+            forward(o, ox, (o + ny - 1) % ny, ox, 11, peer(oy=ny - 1))
+
+    def across(o):
+        for ox in xs:
+            forward(o, 0, o, ox, 10, peer(ox=ox))
 
     def landed(o, ox):
         arrive(big.at[0, o, ox], slot(o, ox))
-
-    def across(i):
-        o = mine_of(i)
-        for ox in xs:
-            forward(o, 0, o, ox, 11, peer(ox=ox))
-
-    def from_x(i):
-        for ox in xs:
-            landed(mine_of(i), ox)
-            upright(i, ox, 12 if i else 13)
-            swap(mine_of(i), ox)
-
-    def from_z(i):
-        o = theirs_of(i)
-        if i:
-            landed(o, 0)
-            swap(o, 0)
-        else:
-            @pl.when(parity == 0)
-            def _():
-                landed(o, 0)
-                swap(o, 0)
-        for ox in xs:
-            landed(o, ox)
-            swap(o, ox)
 
     def unit(c, o):
         fold(big[c, o].reshape(nx * blk, D), True)
@@ -265,13 +239,10 @@
         arrive(big.at[1, o], swap_sem.at[o])
         unit(1, o)
 
-    for i in (2, 1, 3):
-        forward(0, 0, mine_of(i), 0, 9, peer(oy=mine_of(i)))
-
-    @pl.when(parity == 1)
-    def _():
-        forward(0, 0, 1, 0, 10, peer(oy=1))
-
+    for o in far_y:
+        forward(0, 0, o, 0, 9, peer(oy=o))
+    across(0)
+    sideways(0, 0)
     swap(0, 0)
 
     arrive(others(hist_x, nxc), rsem.at[1])
@@ -279,23 +250,22 @@
     for o in range(1, nxc):
         total_h = total_h + hist_x[o]
     hist_z[0] = total_h
-
-    @pl.when(parity == 1)
-    def _():
-        landed(1, 0)
-        upright(0, 0, 14)
-        swap(1, 0)
-
-    across(0)
     for o in range(1, nz):
         send(hist_z.at[0], hist_z.at[o], ssem.at[2], rsem.at[2], peer(oz=o))
-    for i in steps[1:]:
-        landed(mine_of(i), 0)
-        across(i)
-        upright(i, 0, 12)
-        swap(mine_of(i), 0)
-    from_x(0)
-    unit(0, mine_of(0))
+
+    for o in (1, ny - 1):
+        landed(o, 0)
+        swap(o, 0)
+    for ox in xs:
+        landed(0, ox)
+        sideways(0, ox)
+        swap(0, ox)
+    for o in far_y:
+        landed(o, 0)
+        across(o)
+        sideways(o, 0)
+        swap(o, 0)
+    unit(0, 0)
 
     arrive(others(hist_z, nz), rsem.at[2])
     total_h = hist_z[0]
@@ -305,15 +275,26 @@
     for o in range(1, ny):
         send(hist_y.at[0], hist_y.at[o], ssem.at[3], rsem.at[3], peer(oy=o))
 
-    from_x(3)
-    unit(0, mine_of(3))
-    from_z(0)
-    swapped(mine_of(0))
-    from_x(1)
-    unit(0, mine_of(1))
-    from_z(3)
-    unit(0, theirs_of(0))
-    swapped(mine_of(3))
+    for o in (1, ny - 1):
+        for ox in xs:
+            landed(o, ox)
+            swap(o, ox)
+    swapped(0)
+    for o in (3, ny - 3):
+        landed(o, 0)
+        swap(o, 0)
+    unit(0, 1)
+    for o in far_y[:2]:
+        for ox in xs:
+            landed(o, ox)
+            sideways(o, ox)
+            swap(o, ox)
+    unit(0, ny - 1)
+    for ox in xs:
+        landed(4, ox)
+        swap(4, ox)
+    unit(0, 2)
+    swapped(1)
 
     arrive(others(hist_y, ny), rsem.at[3])
     total_h = hist_y[0]
@@ -323,19 +304,19 @@
     for ox, oc in xc_steps:
         send(counts.at[my_xc], counts.at[my_xc], ssem.at[4], rsem.at[4], peer(ox=ox, oc=oc))
 
-    from_x(2)
-    unit(0, mine_of(2))
-    from_z(1)
-    unit(0, theirs_of(3))
-    swapped(theirs_of(0))
-    swapped(mine_of(1))
-    from_z(2)
-    unit(0, theirs_of(1))
-    swapped(theirs_of(3))
-    swapped(mine_of(2))
-    unit(0, theirs_of(2))
-    swapped(theirs_of(1))
-    swapped(theirs_of(2))
+    unit(0, ny - 2)
+    swapped(ny - 1)
+    unit(0, 4)
+    for o in (3, ny - 3):
+        for ox in xs:
+            landed(o, ox)
+            swap(o, ox)
+    for o in far_y:
+        swapped(o)
+    for o in (3, ny - 3):
+        unit(0, o)
+    for o in (3, ny - 3):
+        swapped(o)
 
     best = jnp.maximum(jnp.min(nearest[...], axis=0, keepdims=True) + norms, 0.0)
     mass = jnp.sum(best, axis=1, keepdims=True)
@@ -420,14 +401,8 @@
     drain(others(tot_z, nz), ssem.at[7])
     drain(big.at[1], ssem.at[8])
     drain(big.at[0, 0, pl.ds(0, 3)], ssem.at[9])
-    drain(big.at[0, pl.ds(0, nx - 1)], ssem.at[11])
-    drain(big.at[0, pl.ds(0, 3)], ssem.at[12])
-    drain(big.at[0, 0, pl.ds(0, nx - 1)], ssem.at[13])
-
-    @pl.when(parity == 1)
-    def _():
-        drain(big.at[0, 0, 0], ssem.at[10])
-        drain(big.at[0, 0, 0], ssem.at[14])
+    drain(big.at[0, pl.ds(0, nx - 1)], ssem.at[10])
+    drain(big.at[0, pl.ds(0, 4)], ssem.at[11])
 
 
 def shards(nx, ny, nz, points, centres, picks, assign_pts, cand_assign):
@@ -449,7 +424,7 @@
         pltpu.VMEM((nxc, 1, 128), F32), pltpu.VMEM((ny, 1, 128), F32),
         pltpu.VMEM((nz, 1, 128), F32), dma((5,)),
     ]
-    scratch += [dma((15,)), dma((8,)), dma((nx * ny,)), dma((ny,))]
+    scratch += [dma((12,)), dma((8,)), dma((nx * ny,)), dma((ny,))]
     cost, final = pl.pallas_call(
         functools.partial(kernel, nx, ny, nz, float(1024 * nx * ny * CORES * nz)),
         out_shape=(jax.ShapeDtypeStruct((8, 128), F32), jax.ShapeDtypeStruct((16, D), F32)),

time: 64.9 us -> 60.5 us (0.932)
  Pallas kernels: 60.6 us -> 56.2 us
    pallas_call x1, Pallas kernels: 60.6 us -> 56.2 us  [shards(): pl.pallas_call(functools.partial(kernel, nx, ny, nz, float(1024 * nx * ny...]
where the time goes in v4:
time: 60.5 us; the launch traced here: 59.4 us
  Pallas kernels  56.2 us (93%)
  local copies, waits for them, and re-layouts  2.59 us (4%)
  between operations  0.65 us (1%)
    pallas_call x1, Pallas kernels, shards(): pl.pallas_call(functools.partial(kernel, nx, ny, nz, float(1024 * nx * ny...  56.2 us
    unnamed x4, local copies, waits for them, and re-layouts  2.59 us

profile of v4, /device:TPU:1, one launch (start us, length us, event | category | flops | bytes accessed | tf_op | source)
XLA Modules:
  0.0 59.4 jit_solution(4253392851366531804)
XLA Ops:
  0.6 56.2 %shard_map.68 = (f32[8,128]{1,0:T(8,128)}, f32[16,256]{1,0:T(8,128)}) custom-call(s32[2,1024]{1,0:T(2,128)} %picks_hbm.1, s32[32,128]{1,0:T(8,128)} %bitcast.3, s32[8,128]{1,0:T(8,128)} %bitcast.4, bf16[1024,256]{1,0:T(8,128)(2,1)} %points_hbm.1, bf16[2048,256]{1,0:T(8,128)(2,1)} %centres_hbm.1), custom_call_target="tpu_custom_call" | custom-call | tf_op jit(solution)/shard_map/pallas_call | solution.py:428
  56.8 0.0 copy-start
  56.8 0.7 %copy-done = f32[8,128]{1,0:T(8,128)S(1)} copy-done((f32[8,128]{1,0:T(8,128)S(1)}, f32[8,128]{1,0:T(8,128)}, u32[]{:S(2)}) %copy-start) | copy-done | bytes 4120
  57.5 0.6 copy.9
  58.1 1.3 %copy.10 = f32[16,256]{1,0:T(8,128)} copy(f32[16,256]{1,0:T(8,128)} %get-tuple-element.9) | data formatting | bytes 32768
Async XLA Ops:
  56.8 0.7 %copy-start = (f32[8,128]{1,0:T(8,128)S(1)}, f32[8,128]{1,0:T(8,128)}, u32[]{:S(2)}) copy-start(f32[8,128]{1,0:T(8,128)} %get-tuple-element.4) | copy-start | bytes 12292

commit v5 on v4

--- a/solution.py
+++ b/solution.py
@@ -37,7 +37,7 @@
            cost_ref, final_ref,
            picks_ref, owner_ref, assign_ref, pts, pts2, cen, picked, zbuf, big, nearest, meta,
            hist, hist_x, hist_z, hist_y, counts,
-           tot_x, tot_y, tot_z, local_sem, ssem, rsem, block_sem, swap_sem):
+           tot_p, tot_z, local_sem, ssem, rsem, block_sem, swap_sem):
     row = lax.axis_index("row")
     z = lax.axis_index("col")
     core = lax.rem(row, CORES)
@@ -82,8 +82,10 @@
 
     xc_steps = [(ox, oc) for ox in range(nx) for oc in range(CORES) if ox or oc]
     barrier = pltpu.get_barrier_semaphore()
-    peers = [peer(oz=o) for o in range(1, nz)] + [peer(oy=o) for o in range(1, ny)]
-    peers += [peer(ox=ox, oc=oc) for ox, oc in xc_steps]
+    plane = [(ox, oy, oc) for ox in range(nx) for oy in range(ny) for oc in range(CORES)][1:]
+    plane.sort(key=lambda p: -min(p[0], nx - p[0]) - min(p[1], ny - p[1]))
+    plane_peers = [peer(ox=ox, oy=oy, oc=oc) for ox, oy, oc in plane]
+    peers = [peer(oz=o) for o in range(1, nz)] + plane_peers
     for other in peers:
         pl.semaphore_signal(barrier, inc=1, device_id=other, device_id_type=MESH)
 
@@ -208,6 +210,7 @@
     big[0, 0, 0] = packed.astype(BF16)
 
     xs = near_first(nx)
+    near_x = (1, nx - 1)
     far_y = (2, ny - 2, 4)
 
     def slot(o, ox):
@@ -220,6 +223,8 @@
         send(big.at[0, o, ox], big.at[1, o, ox], ssem.at[8], swap_sem.at[o], peer(oc=1))
 
     def sideways(o, ox):
+        if o == 0 and ox in near_x:
+            return
         if o == 0 or o == 2:
             forward(o, ox, o + 1, ox, 11, peer(oy=1))
         if o == 0 or o == ny - 2:
@@ -255,6 +260,8 @@
 
     for o in (1, ny - 1):
         landed(o, 0)
+        for ox in near_x:
+            forward(o, 0, o, ox, 10, peer(ox=ox))
         swap(o, 0)
     for ox in xs:
         landed(0, ox)
@@ -326,10 +333,7 @@
             send(buf.at[0], buf.at[o + 1], ssem.at[sem], rsem.at[sem], device)
         between()
         arrive(others(buf, len(devices) + 1), rsem.at[sem])
-        result = buf[0]
-        for o in range(len(devices)):
-            result = result + buf[o + 1]
-        return result
+        return jnp.sum(buf[...], axis=0)
 
     targets = row * (K_FINAL // (nx * ny * CORES)) + lax.broadcasted_iota(I32, (16, 128), 0)
     state = {}
@@ -382,9 +386,12 @@
                 num = num + product(member[:, :blk], big[c, o, ox])
         state["num"], state["den"] = num, den
 
-    tot_x[0] = jnp.broadcast_to(mass, (1, 128))
-    tot_y[0] = stage(tot_x, 5, [peer(ox=ox, oc=oc) for ox, oc in xc_steps], lloyd_centres)
-    tot_z[0] = stage(tot_y, 6, [peer(oy=o) for o in range(1, ny)], lambda: lloyd_slots(0))
+    def lloyd_first():
+        lloyd_centres()
+        lloyd_slots(0)
+
+    tot_p[0] = jnp.broadcast_to(mass, (1, 128))
+    tot_z[0] = stage(tot_p, 5, plane_peers, lloyd_first)
     total = stage(tot_z, 7, [peer(oz=o) for o in range(1, nz)], lambda: lloyd_slots(1))
     den = jnp.sum(state["den"], axis=1, keepdims=True)
     final_ref[...] = state["num"] / den
@@ -396,13 +403,17 @@
     drain(others(hist_z, nz), ssem.at[2])
     drain(others(hist_y, ny), ssem.at[3])
     drain(others(counts, nxc), ssem.at[4])
-    drain(others(tot_x, nxc), ssem.at[5])
-    drain(others(tot_y, ny), ssem.at[6])
+    drain(others(tot_p, nxc * ny), ssem.at[5])
     drain(others(tot_z, nz), ssem.at[7])
     drain(big.at[1], ssem.at[8])
     drain(big.at[0, 0, pl.ds(0, 3)], ssem.at[9])
-    drain(big.at[0, pl.ds(0, nx - 1)], ssem.at[10])
-    drain(big.at[0, pl.ds(0, 4)], ssem.at[11])
+    drain(big.at[0, pl.ds(0, 4)], ssem.at[10])
+    drain(big.at[0, pl.ds(0, 3)], ssem.at[11])
+
+
+def hand_over(cost_ref, final_ref, cost_out, final_out):
+    cost_out[...] = cost_ref[...]
+    final_out[...] = final_ref[...]
 
 
 def shards(nx, ny, nz, points, centres, picks, assign_pts, cand_assign):
@@ -421,8 +432,7 @@
         pltpu.VMEM((nxc, per, 128), F32), pltpu.VMEM((nxc, per, 128), F32),
         pltpu.VMEM((nz, per, 128), F32), pltpu.VMEM((ny, per, 128), F32),
         pltpu.VMEM((nxc, per, 128), F32),
-        pltpu.VMEM((nxc, 1, 128), F32), pltpu.VMEM((ny, 1, 128), F32),
-        pltpu.VMEM((nz, 1, 128), F32), dma((5,)),
+        pltpu.VMEM((nxc * ny, 1, 128), F32), pltpu.VMEM((nz, 1, 128), F32), dma((5,)),
     ]
     scratch += [dma((12,)), dma((8,)), dma((nx * ny,)), dma((ny,))]
     cost, final = pl.pallas_call(
@@ -434,6 +444,10 @@
         compiler_params=pltpu.CompilerParams(
             collective_id=0, has_side_effects=True, vmem_limit_bytes=60 << 20),
     )(picks, cand_assign.reshape(32, 128), assign_pts.reshape(8, 128), points, centres)
+    cost, final = pl.pallas_call(
+        hand_over,
+        out_shape=(jax.ShapeDtypeStruct((8, 128), F32), jax.ShapeDtypeStruct((16, D), F32)),
+    )(cost, final)
     return cost.reshape(1024), final
 
 

time: 60.5 us -> 58.4 us (0.965); the launches traced: 59.4 us -> 58.2 us
  local copies, waits for them, and re-layouts: 2.59 us -> 0 us
  Pallas kernels: 56.2 us -> 57.6 us
    unnamed x4 -> x0, local copies, waits for them, and re-layouts: 2.59 us -> none
    pallas_call x0 -> x1, Pallas kernels: none -> 1.33 us  [shards(): pl.pallas_call(hand_over, out_shape=(jax.ShapeDtypeStruct((8, 128), F32),...]
where the time goes in v5:
time: 58.4 us; the launch traced here: 58.2 us
  Pallas kernels  57.6 us (99%)
  between operations  0.64 us (1%)
    pallas_call x1, Pallas kernels, shards(): pl.pallas_call(functools.partial(kernel, nx, ny, nz, float(1024 * nx * ny...  56.2 us
    pallas_call x1, Pallas kernels, shards(): pl.pallas_call(hand_over, out_shape=(jax.ShapeDtypeStruct((8, 128), F32),...  1.33 us

profile of v5, /device:TPU:1, one launch (start us, length us, event | category | flops | bytes accessed | tf_op | source)
XLA Modules:
  0.0 58.2 jit_solution(10682829600758774642)
XLA Ops:
  0.6 56.2 %shard_map.68 = (f32[8,128]{1,0:T(8,128)}, f32[16,256]{1,0:T(8,128)}) custom-call(s32[2,1024]{1,0:T(2,128)} %picks_hbm.1, s32[32,128]{1,0:T(8,128)} %bitcast.3, s32[8,128]{1,0:T(8,128)} %bitcast.4, bf16[1024,256]{1,0:T(8,128)(2,1)} %points_hbm.1, bf16[2048,256]{1,0:T(8,128)(2,1)} %centres_hbm.1), custom_call_target="tpu_custom_call" | custom-call | tf_op jit(solution)/shard_map/pallas_call | solution.py:438
  56.9 1.3 %shard_map.69 = (f32[8,128]{1,0:T(8,128)}, f32[16,256]{1,0:T(8,128)}) custom-call(f32[8,128]{1,0:T(8,128)} %get-tuple-element.6.cost_ref, f32[16,256]{1,0:T(8,128)} %get-tuple-element.7.final_ref), custom_call_target="tpu_custom_call" | custom-call | tf_op jit(solution)/shard_map/pallas_call | solution.py:447

commit v6 on v5

--- a/solution.py
+++ b/solution.py
@@ -35,7 +35,7 @@
 def kernel(nx, ny, nz, npts,
            picks_hbm, owner_hbm, assign_hbm, points_hbm, centres_hbm,
            cost_ref, final_ref,
-           picks_ref, owner_ref, assign_ref, pts, pts2, cen, picked, zbuf, big, nearest, meta,
+           picks_ref, owner_ref, assign_ref, first_rows, pts, pts2, cen, picked, zbuf, big, nearest, meta,
            hist, hist_x, hist_z, hist_y, counts,
            tot_p, tot_z, local_sem, ssem, rsem, block_sem, swap_sem):
     row = lax.axis_index("row")
@@ -76,7 +76,7 @@
 
     loads = [pltpu.make_async_copy(src, dst, local_sem.at[i]) for i, (src, dst) in enumerate(
         [(picks_hbm, picks_ref), (owner_hbm, owner_ref), (points_hbm, pts),
-         (centres_hbm, cen), (assign_hbm, assign_ref)])]
+         (centres_hbm.at[pl.ds(0, 16)], first_rows), (centres_hbm, cen), (assign_hbm, assign_ref)])]
     for load in loads:
         load.start()
 
@@ -85,7 +85,7 @@
     plane = [(ox, oy, oc) for ox in range(nx) for oy in range(ny) for oc in range(CORES)][1:]
     plane.sort(key=lambda p: -min(p[0], nx - p[0]) - min(p[1], ny - p[1]))
     plane_peers = [peer(ox=ox, oy=oy, oc=oc) for ox, oy, oc in plane]
-    peers = [peer(oz=o) for o in range(1, nz)] + plane_peers
+    peers = [peer(oz=o) for o in near_first(nz)[::-1]] + plane_peers
     for other in peers:
         pl.semaphore_signal(barrier, inc=1, device_id=other, device_id_type=MESH)
 
@@ -129,13 +129,12 @@
     digit_c = (code_row >> 16).astype(F32)
     loads[2].wait()
     loads[3].wait()
-    loads[4].wait()
     mine = jnp.dot(choose16, pts[...], preferred_element_type=F32)[:8, :]
     slot_col = lax.broadcasted_iota(I32, (8, D), 0)
     filled = jnp.zeros((8, D), I32)
     for s in range(slots):
         filled = jnp.where(slot_col == s, jnp.broadcast_to(local_ids[s], (8, D)), filled)
-    spare = jnp.broadcast_to(cen[0:16, :].astype(F32)[0:1, :], (8, D))
+    spare = jnp.broadcast_to(first_rows[...].astype(F32)[0:1, :], (8, D))
     mine = jnp.where(filled >= FAR, spare, mine)
     row_six = jnp.concatenate([digit_a, digit_b], axis=1)
     row_seven = jnp.concatenate([digit_c, digit_c], axis=1)
@@ -148,6 +147,8 @@
     for o in near_first(nz)[::-1]:
         send(zbuf.at[z], zbuf.at[z], ssem.at[0], rsem.at[0], peer(oz=o))
 
+    loads[4].wait()
+    loads[5].wait()
     acc = jnp.zeros((32, 128), F32)
     hi_iota = lax.broadcasted_iota(I32, (32, 128), 0)
     lo_iota = lax.broadcasted_iota(I32, (128, 128), 0)
@@ -193,6 +194,13 @@
 
     lax.fori_loop(0, cen.shape[0] // 512, fold_centres, 0)
 
+    srow = lax.broadcasted_iota(I32, (blk, nz * 8), 0)
+    scol = lax.broadcasted_iota(I32, (blk, nz * 8), 1)
+    sdev = (srow * 43691) >> 18
+    pick = (scol == sdev * 8 + (srow - sdev * slots)) & (srow < rows)
+    pick = pick | ((srow == rows) & ((scol & 7) == slots))
+    pick = pick | ((srow == rows + 1) & ((scol & 7) == slots + 1))
+    choose_rows = jnp.where(pick, 1.0, 0.0).astype(BF16)
     arrive(others(zbuf, nz), rsem.at[0])
     column = jnp.concatenate([zbuf[i].astype(F32) for i in range(nz)], axis=0)
     crow = lax.broadcasted_iota(I32, column.shape, 0)
@@ -200,17 +208,10 @@
     cdev = (clane * 43691) >> 18
     drop = ((crow & 7) >= slots) & ((crow >> 3) != cdev)
     column = jnp.where(drop, 0.0, column).astype(BF16)
-    srow = lax.broadcasted_iota(I32, (blk, nz * 8), 0)
-    scol = lax.broadcasted_iota(I32, (blk, nz * 8), 1)
-    sdev = (srow * 43691) >> 18
-    pick = (scol == sdev * 8 + (srow - sdev * slots)) & (srow < rows)
-    pick = pick | ((srow == rows) & ((scol & 7) == slots))
-    pick = pick | ((srow == rows + 1) & ((scol & 7) == slots + 1))
-    packed = jnp.dot(jnp.where(pick, 1.0, 0.0).astype(BF16), column, preferred_element_type=F32)
+    packed = jnp.dot(choose_rows, column, preferred_element_type=F32)
     big[0, 0, 0] = packed.astype(BF16)
 
     xs = near_first(nx)
-    near_x = (1, nx - 1)
     far_y = (2, ny - 2, 4)
 
     def slot(o, ox):
@@ -223,8 +224,6 @@
         send(big.at[0, o, ox], big.at[1, o, ox], ssem.at[8], swap_sem.at[o], peer(oc=1))
 
     def sideways(o, ox):
-        if o == 0 and ox in near_x:
-            return
         if o == 0 or o == 2:
             forward(o, ox, o + 1, ox, 11, peer(oy=1))
         if o == 0 or o == ny - 2:
@@ -260,8 +259,6 @@
 
     for o in (1, ny - 1):
         landed(o, 0)
-        for ox in near_x:
-            forward(o, 0, o, ox, 10, peer(ox=ox))
         swap(o, 0)
     for ox in xs:
         landed(0, ox)
@@ -407,8 +404,8 @@
     drain(others(tot_z, nz), ssem.at[7])
     drain(big.at[1], ssem.at[8])
     drain(big.at[0, 0, pl.ds(0, 3)], ssem.at[9])
-    drain(big.at[0, pl.ds(0, 4)], ssem.at[10])
-    drain(big.at[0, pl.ds(0, 3)], ssem.at[11])
+    drain(big.at[0, pl.ds(0, 3)], ssem.at[10])
+    drain(big.at[0, pl.ds(0, 4)], ssem.at[11])
 
 
 def hand_over(cost_ref, final_ref, cost_out, final_out):
@@ -425,6 +422,7 @@
     hbm = pl.BlockSpec(memory_space=pltpu.MemorySpace.HBM)
     scratch = [
         pltpu.VMEM(picks.shape, I32), pltpu.VMEM((32, 128), I32), pltpu.VMEM((8, 128), I32),
+        pltpu.VMEM((16, D), BF16),
         pltpu.VMEM(points.shape, BF16), pltpu.VMEM(points.shape, BF16),
         pltpu.VMEM(centres.shape, BF16), pltpu.VMEM((16, 128), I32),
         pltpu.VMEM((nz, 8, D), BF16), pltpu.VMEM((CORES, ny, nx, blk, D), BF16),
@@ -432,7 +430,7 @@
         pltpu.VMEM((nxc, per, 128), F32), pltpu.VMEM((nxc, per, 128), F32),
         pltpu.VMEM((nz, per, 128), F32), pltpu.VMEM((ny, per, 128), F32),
         pltpu.VMEM((nxc, per, 128), F32),
-        pltpu.VMEM((nxc * ny, 1, 128), F32), pltpu.VMEM((nz, 1, 128), F32), dma((5,)),
+        pltpu.VMEM((nxc * ny, 1, 128), F32), pltpu.VMEM((nz, 1, 128), F32), dma((6,)),
     ]
     scratch += [dma((12,)), dma((8,)), dma((nx * ny,)), dma((ny,))]
     cost, final = pl.pallas_call(

time: 58.4 us -> 58.1 us (level)
  no operation moved by 1% of the time
where the time goes in v6:
time: 58.1 us; the launch traced here: 57.9 us
  Pallas kernels  57.2 us (98%)
  between operations  0.64 us (1%)
    pallas_call x1, Pallas kernels, shards(): pl.pallas_call(functools.partial(kernel, nx, ny, nz, float(1024 * nx * ny...  55.9 us
    pallas_call x1, Pallas kernels, shards(): pl.pallas_call(hand_over, out_shape=(jax.ShapeDtypeStruct((8, 128), F32),...  1.33 us

profile of v6, /device:TPU:1, one launch (start us, length us, event | category | flops | bytes accessed | tf_op | source)
XLA Modules:
  0.0 57.9 jit_solution(15435218533723003776)
XLA Ops:
  0.6 55.9 %shard_map.68 = (f32[8,128]{1,0:T(8,128)}, f32[16,256]{1,0:T(8,128)}) custom-call(s32[2,1024]{1,0:T(2,128)} %picks_hbm.1, s32[32,128]{1,0:T(8,128)} %bitcast.3, s32[8,128]{1,0:T(8,128)} %bitcast.4, bf16[1024,256]{1,0:T(8,128)(2,1)} %points_hbm.1, bf16[2048,256]{1,0:T(8,128)(2,1)} %centres_hbm.1), custom_call_target="tpu_custom_call" | custom-call | tf_op jit(solution)/shard_map/pallas_call | solution.py:436
  56.5 1.3 %shard_map.69 = (f32[8,128]{1,0:T(8,128)}, f32[16,256]{1,0:T(8,128)}) custom-call(f32[8,128]{1,0:T(8,128)} %get-tuple-element.6.cost_ref, f32[16,256]{1,0:T(8,128)} %get-tuple-element.7.final_ref), custom_call_target="tpu_custom_call" | custom-call | tf_op jit(solution)/shard_map/pallas_call | solution.py:445

commit v7 on v5

--- a/solution.py
+++ b/solution.py
@@ -314,12 +314,12 @@
     unit(0, ny - 2)
     swapped(ny - 1)
     unit(0, 4)
+    for o in far_y:
+        swapped(o)
     for o in (3, ny - 3):
         for ox in xs:
             landed(o, ox)
             swap(o, ox)
-    for o in far_y:
-        swapped(o)
     for o in (3, ny - 3):
         unit(0, o)
     for o in (3, ny - 3):

time: 58.4 us -> 57.7 us (0.988)
  Pallas kernels: 57.6 us -> 56.9 us
    pallas_call x1, Pallas kernels: 56.2 us -> 55.6 us  [shards(): pl.pallas_call(functools.partial(kernel, nx, ny, nz, float(1024 * nx * ny...]
where the time goes in v7:
time: 57.7 us; the launch traced here: 57.5 us
  Pallas kernels  56.9 us (99%)
  between operations  0.64 us (1%)
    pallas_call x1, Pallas kernels, shards(): pl.pallas_call(functools.partial(kernel, nx, ny, nz, float(1024 * nx * ny...  55.6 us
    pallas_call x1, Pallas kernels, shards(): pl.pallas_call(hand_over, out_shape=(jax.ShapeDtypeStruct((8, 128), F32),...  1.33 us

profile of v7, /device:TPU:1, one launch (start us, length us, event | category | flops | bytes accessed | tf_op | source)
XLA Modules:
  0.0 57.5 jit_solution(16152806604529638857)
XLA Ops:
  0.6 55.6 %shard_map.68 = (f32[8,128]{1,0:T(8,128)}, f32[16,256]{1,0:T(8,128)}) custom-call(s32[2,1024]{1,0:T(2,128)} %picks_hbm.1, s32[32,128]{1,0:T(8,128)} %bitcast.3, s32[8,128]{1,0:T(8,128)} %bitcast.4, bf16[1024,256]{1,0:T(8,128)(2,1)} %points_hbm.1, bf16[2048,256]{1,0:T(8,128)(2,1)} %centres_hbm.1), custom_call_target="tpu_custom_call" | custom-call | tf_op jit(solution)/shard_map/pallas_call | solution.py:438
  56.2 1.3 %shard_map.69 = (f32[8,128]{1,0:T(8,128)}, f32[16,256]{1,0:T(8,128)}) custom-call(f32[8,128]{1,0:T(8,128)} %get-tuple-element.6.cost_ref, f32[16,256]{1,0:T(8,128)} %get-tuple-element.7.final_ref), custom_call_target="tpu_custom_call" | custom-call | tf_op jit(solution)/shard_map/pallas_call | solution.py:447
